TPU v7x, 32 devices: a whole 2x2x4 slice. The times are simulated.
32 devices in a mesh: head: 2 (over y), ctx: 4 (over z), batch: 4 (over x, core).
Axes of the slice: x: 2, y: 2, z: 4, core: 2. Of those that a mesh axis runs over, the one named last changes fastest.
Arguments:
- tokens: bfloat16 [4, 1024, 1024], P('batch', ('ctx', 'head')), may hold values from -6 to 6
- cotangent: bfloat16 [4, 1024, 1024], P('batch', ('ctx', 'head')), may hold values from -6 to 6
- norm1_gain: bfloat16 [1024], P(('head', 'ctx', 'batch')), may hold values from 0.5 to 1.5
- w_query: bfloat16 [1024, 1024], P(('head', 'ctx', 'batch')), may hold values from -0.1875 to 0.1875
- w_key: bfloat16 [1024, 1024], P(('head', 'ctx', 'batch')), may hold values from -0.1875 to 0.1875
- w_value: bfloat16 [1024, 2048], P(('head', 'ctx', 'batch')), may hold values from -0.1875 to 0.1875
- w_gate: bfloat16 [1024, 2048], P(('head', 'ctx', 'batch')), may hold values from -0.1875 to 0.1875
- w_rates: bfloat16 [1024, 16], P(('head', 'ctx', 'batch')), may hold values from -0.1875 to 0.1875
- conv_query: bfloat16 [4, 1024], P(None, 'head'), may hold values from -3 to 3
- conv_key: bfloat16 [4, 1024], P(None, 'head'), may hold values from -3 to 3
- conv_value: bfloat16 [4, 2048], P(None, 'head'), may hold values from -3 to 3
- decay_log: float32 [8], P('head'), may hold values from -7 to 0.5
- decay_bias: float32 [8], P('head'), may hold values from -4 to 1
- out_gain: bfloat16 [2048], P('head'), may hold values from 0.5 to 1.5
- w_out: bfloat16 [1024, 2048], P(('head', 'ctx', 'batch')), may hold values from -0.125 to 0.125
- norm2_gain: bfloat16 [1024], P(('head', 'ctx', 'batch')), may hold values from 0.5 to 1.5
- w_ffgate: bfloat16 [1024, 2816], P(('head', 'ctx', 'batch')), may hold values from -0.1875 to 0.1875
- w_ffup: bfloat16 [1024, 2816], P(('head', 'ctx', 'batch')), may hold values from -0.1875 to 0.1875
- w_down: bfloat16 [1024, 2816], P(('head', 'ctx', 'batch')), may hold values from -0.109375 to 0.109375
Outputs:
- output: bfloat16 [4, 1024, 1024], P('batch', ('ctx', 'head'))
- input_grad: float32 [4, 1024, 1024], P('batch', ('ctx', 'head'))
- g_norm1: float32 [1024], P(('head', 'ctx', 'batch'))
- g_query: float32 [1024, 1024], P(('ctx', 'batch'), 'head')
- g_key: float32 [1024, 1024], P(('ctx', 'batch'), 'head')
- g_value: float32 [1024, 2048], P(('ctx', 'batch'), 'head')
- g_gate: float32 [1024, 2048], P(('ctx', 'batch'), 'head')
- g_rates: float32 [1024, 16], P(('ctx', 'batch'), 'head')
- g_conv_query: float32 [4, 1024], P(None, 'head')
- g_conv_key: float32 [4, 1024], P(None, 'head')
- g_conv_value: float32 [4, 2048], P(None, 'head')
- g_decay_log: float32 [8], P('head')
- g_decay_bias: float32 [8], P('head')
- g_out_gain: float32 [2048], P('head')
- g_out: float32 [1024, 2048], P(('ctx', 'batch'), 'head')
- g_norm2: float32 [1024], P(('head', 'ctx', 'batch'))
- g_ffgate: float32 [1024, 2816], P(('ctx', 'batch'), 'head')
- g_ffup: float32 [1024, 2816], P(('ctx', 'batch'), 'head')
- g_down: float32 [1024, 2816], P(('ctx', 'batch'), 'head')
All inputs are finite; a program needn't handle non-finite values.
Results may differ from a plain program's by a relative error of at most 0.02.
Values may be sent and summed in bfloat16 or wider, within the bound.
A program may use at most 256 MiB of HBM per device.

v0:
```python
import math

import jax
import jax.numpy as jnp
from jax import lax
from jax.experimental import pallas as pl
from jax.experimental.pallas import tpu as pltpu
from jax.sharding import PartitionSpec as P

KW = 4
CHUNK = 256
epsilon = 1e-06
highest_precision = lax.Precision.HIGHEST


def passed_along(block, axis, distance):
    devices = range(lax.axis_size(axis))
    route = [(i - distance, i) for i in devices if i - distance in devices]
    return lax.ppermute(block, axis, route)


def product(first, second, first_dim, second_dim):
    return lax.dot_general(
        first,
        second,
        (((first_dim,), (second_dim,)), ((), ())),
        precision=highest_precision,
        preferred_element_type=jnp.float32,
    )


@jax.custom_vjp
def mul_nn(first, second):
    return product(first, second, 1, 0)


@jax.custom_vjp
def mul_nt(first, second):
    return product(first, second, 1, 1)


@jax.custom_vjp
def mul_tn(first, second):
    return product(first, second, 0, 0)


mul_nn.defvjp(
    lambda a, b: (product(a, b, 1, 0), (a, b)),
    lambda res, ct: (product(ct, res[1], 1, 1), product(res[0], ct, 0, 0)),
)
mul_nt.defvjp(
    lambda a, b: (product(a, b, 1, 1), (a, b)),
    lambda res, ct: (product(ct, res[1], 1, 0), product(ct, res[0], 0, 0)),
)
mul_tn.defvjp(
    lambda a, b: (product(a, b, 0, 0), (a, b)),
    lambda res, ct: (product(res[1], ct, 1, 1), product(res[0], ct, 1, 0)),
)


@jax.custom_vjp
def solve_with(inverse, lower, rhs):
    return product(inverse, rhs, 1, 0)


def solve_forward(inverse, lower, rhs):
    solved = product(inverse, rhs, 1, 0)
    return solved, (inverse, solved)


def solve_backward(res, ct):
    inverse, solved = res
    rhs_grad = product(inverse, ct, 0, 0)
    return jnp.zeros_like(inverse), -product(rhs_grad, solved, 1, 1), rhs_grad


solve_with.defvjp(solve_forward, solve_backward)


def square_masks(size):
    rows = lax.broadcasted_iota(jnp.int32, (size, size), 0)
    cols = lax.broadcasted_iota(jnp.int32, (size, size), 1)
    return rows, cols


def unit_lower_inverse(lower):
    size = lower.shape[0]
    rows, cols = square_masks(size)
    inverse = jnp.where(rows == cols, 1.0, 0.0).astype(jnp.float32)
    level = 0
    while (1 << level) < size:
        width = 1 << level
        joined = (rows // (2 * width)) == (cols // (2 * width))
        mask = joined & ((rows // width) > (cols // width))
        off = jnp.where(mask, lower, 0.0)
        if level == 0:
            inverse = inverse - off
        else:
            inverse = inverse - product(product(inverse, off, 1, 0), inverse, 1, 0)
        level += 1
    return inverse


def silu_rows(x):
    return x * lax.logistic(x)


def unit_rows(matrix):
    return matrix * lax.rsqrt(jnp.sum(matrix * matrix, axis=1, keepdims=True) + epsilon)


def piece_terms(query_in, key_in, value_in, decay, strength, nn, nt):
    size = query_in.shape[0]
    width = query_in.shape[1]
    rows, cols = square_masks(size)
    strict = rows > cols
    inclusive = rows >= cols
    ones_low = jnp.where(inclusive, 1.0, 0.0).astype(jnp.float32)
    ones_high = jnp.where(rows < cols, 1.0, 0.0).astype(jnp.float32)
    queries = unit_rows(silu_rows(query_in)) * (1.0 / math.sqrt(width))
    keys = unit_rows(silu_rows(key_in))
    values = silu_rows(value_in)
    gaps = nn(ones_low, jnp.where(strict, jnp.broadcast_to(decay, (size, size)), 0.0))
    spread = jnp.exp(gaps)
    decay_wide = jnp.broadcast_to(decay, (size, width))
    head_decay = jnp.exp(nn(ones_low, decay_wide))
    tail_decay = jnp.exp(nn(ones_high, decay_wide))
    final = jnp.exp(jnp.sum(decay, axis=0, keepdims=True))
    lower = jnp.where(strict, spread * nt(keys, keys), 0.0) * strength
    scores = jnp.where(inclusive, spread * nt(queries, keys), 0.0)
    return (
        lower,
        scores,
        head_decay * queries,
        head_decay * keys,
        tail_decay * keys,
        values,
        final,
    )


def plain_nn(a, b):
    return product(a, b, 1, 0)


def plain_nt(a, b):
    return product(a, b, 1, 1)


def forward_kernel(q_ref, k_ref, v_ref, d_ref, s_ref, x_ref, o_ref, e_ref, m_ref, f_ref):
    strength = s_ref[...]
    lower, scores, led_queries, led_keys, tail_keys, values, final = piece_terms(
        q_ref[...], k_ref[...], v_ref[...], d_ref[...], strength, plain_nn, plain_nt
    )
    inverse = unit_lower_inverse(lower)
    x_ref[...] = inverse
    direct = product(inverse, strength * values, 1, 0)
    across = product(inverse, strength * led_keys, 1, 0)
    o_ref[...] = product(scores, direct, 1, 0)
    e_ref[...] = led_queries - product(scores, across, 1, 0)
    width = led_keys.shape[1]
    rows, cols = square_masks(width)
    m_ref[...] = jnp.where(rows == cols, jnp.broadcast_to(final, (width, width)), 0.0) - product(
        tail_keys, across, 0, 0
    )
    f_ref[...] = product(tail_keys, direct, 0, 0)


def backward_kernel(
    q_ref, k_ref, v_ref, d_ref, s_ref, x_ref, i_ref, g_ref, t_ref,
    dq_ref, dk_ref, dv_ref, dd_ref, ds_ref,
):
    inverse = x_ref[...]
    start = i_ref[...]

    def run(query_in, key_in, value_in, decay, strength):
        lower, scores, led_queries, led_keys, tail_keys, values, final = piece_terms(
            query_in, key_in, value_in, decay, strength, mul_nn, mul_nt
        )
        update = solve_with(inverse, lower, strength * (values - mul_nn(led_keys, start)))
        mixed = mul_nn(led_queries, start) + mul_nn(scores, update)
        last = final * start + mul_tn(tail_keys, update)
        return mixed, last

    unused, pull = jax.vjp(run, q_ref[...], k_ref[...], v_ref[...], d_ref[...], s_ref[...])
    grads = pull((g_ref[...], t_ref[...]))
    for ref, grad in zip((dq_ref, dk_ref, dv_ref, dd_ref, ds_ref), grads):
        ref[...] = grad


def out_gate(mixer_rows, gate_rows, gain_row):
    scale = lax.rsqrt(jnp.mean(mixer_rows * mixer_rows, axis=1, keepdims=True) + epsilon)
    return mixer_rows * scale * gain_row * silu_rows(gate_rows)


def gate_kernel(o_ref, e_ref, i_ref, gate_ref, gain_ref, out_ref):
    mixer_rows = o_ref[...] + product(e_ref[...], i_ref[...], 1, 0)
    gated = out_gate(mixer_rows, gate_ref[...].astype(jnp.float32), gain_ref[...])
    out_ref[...] = gated.astype(out_ref.dtype)


def gate_back_kernel(
    o_ref, e_ref, i_ref, gate_ref, gain_ref, grad_ref, mg_ref, gg_ref, ng_ref, r_ref
):
    effect = e_ref[...]
    mixer_rows = o_ref[...] + product(effect, i_ref[...], 1, 0)
    unused, pull = jax.vjp(
        out_gate, mixer_rows, gate_ref[...].astype(jnp.float32), gain_ref[...]
    )
    mixer_grad, gate_grad, gain_grad = pull(grad_ref[...].astype(jnp.float32))
    mg_ref[...] = mixer_grad
    gg_ref[...] = gate_grad.astype(gg_ref.dtype)
    ng_ref[...] = gain_grad
    r_ref[...] = product(effect, mixer_grad, 0, 0)


def per_head(kernel, grid, ins, outs, args, flops):
    return pl.pallas_call(
        kernel,
        grid=grid,
        in_specs=ins,
        out_specs=[spec for spec, _ in outs],
        out_shape=[shape for _, shape in outs],
        cost_estimate=pl.CostEstimate(
            flops=flops, bytes_accessed=sum(a.size * a.dtype.itemsize for a in args), transcendentals=0
        ),
    )(*args)


def columns(rows, width, first):
    return pl.BlockSpec((rows, width), lambda h, c, first=first: (c, first + h))


def heads_spec(*shape):
    return pl.BlockSpec((None, None) + shape, lambda h, c: (h, c) + (0,) * len(shape))


def of_shape(shape, kind=jnp.float32):
    return jax.ShapeDtypeStruct(shape, kind)


def state_product(state_map, held):
    return jnp.einsum("hij,hjv->hiv", state_map, held, precision=highest_precision)


def state_pull(state_map, held):
    return jnp.einsum("hji,hjv->hiv", state_map, held, precision=highest_precision)


def mat_nt(first_mat, second_mat):
    return lax.dot_general(
        first_mat, second_mat, (((1,), (1,)), ((), ())), preferred_element_type=jnp.float32
    )


def mat_tn(first_mat, second_mat):
    return lax.dot_general(
        first_mat, second_mat, (((0,), (0,)), ((), ())), preferred_element_type=jnp.float32
    )


def mat_nn(first_mat, second_mat):
    return jnp.dot(first_mat, second_mat, preferred_element_type=jnp.float32)


def rms_scale(hidden, gain_vec):
    return (
        hidden * lax.rsqrt(jnp.mean(hidden * hidden, axis=-1, keepdims=True) + epsilon) * gain_vec
    )


def swiglu(gate_part, up_part):
    return jax.nn.silu(gate_part) * up_part


def short_conv(padded, conv_all):
    length = padded.shape[0] - (KW - 1)
    mixed_rows = padded[0:length] * conv_all[0]
    for tap_index in range(1, KW):
        mixed_rows = mixed_rows + padded[tap_index : tap_index + length] * conv_all[tap_index]
    return mixed_rows


def decay_rates(rates, decay_log, decay_bias):
    heads = decay_log.shape[0]
    pairs = jnp.transpose(rates.reshape(rates.shape[0], heads, 2), (2, 1, 0))
    log_decay = -jnp.exp(decay_log)[:, None] * jax.nn.softplus(pairs[0] + decay_bias[:, None])
    strength = jax.nn.sigmoid(pairs[1])
    return log_decay[:, :, None], strength[:, :, None]


def split_columns(matrix, widths):
    pieces = []
    offset_col = 0
    for width_one in widths:
        pieces.append(matrix[:, offset_col : offset_col + width_one])
        offset_col = offset_col + width_one
    return pieces


def head_halves(weights, parts):
    slabs = []
    for part in range(parts):
        cut = []
        for weight in weights:
            width = weight.shape[1] // parts
            cut.append(weight[:, part * width : (part + 1) * width])
        slabs.append(jnp.concatenate(cut, axis=1))
    return jnp.stack(slabs)


def swap_halves(slabs):
    return lax.all_to_all(slabs, "head", split_axis=0, concat_axis=0, tiled=True)


def whole_rows(slabs):
    full = lax.all_gather(slabs, ("ctx", "batch"), axis=1, tiled=True)
    return full.reshape(full.shape[0] * full.shape[1], full.shape[2])


def other_parts(block):
    parts = lax.axis_size("head")
    total = None
    for shift in range(1, parts):
        moved = lax.ppermute(block, "head", [(i, (i + shift) % parts) for i in range(parts)])
        moved = moved.astype(jnp.float32)
        total = moved if total is None else total + moved
    return total


def head_sum(partial, kind=jnp.bfloat16):
    sent = partial.astype(kind)
    if lax.axis_size("head") == 1:
        return sent.astype(jnp.float32)
    return sent.astype(jnp.float32) + other_parts(sent)


def own_rows_sum(partial):
    parts = lax.axis_size("head")
    rows = partial.shape[0] // parts
    me = lax.axis_index("head")
    total = lax.dynamic_slice_in_dim(partial, me * rows, rows, 0)
    for shift in range(1, parts):
        target = lax.rem(me + shift, parts)
        sent = lax.dynamic_slice_in_dim(partial, target * rows, rows, 0).astype(jnp.bfloat16)
        route = [(i, (i + shift) % parts) for i in range(parts)]
        total = total + lax.ppermute(sent, "head", route).astype(jnp.float32)
    return total


def body(
    tokens,
    cotangent,
    norm1_gain,
    w_query,
    w_key,
    w_value,
    w_gate,
    w_rates,
    conv_query,
    conv_key,
    conv_value,
    decay_log,
    decay_bias,
    out_gain,
    w_out,
    norm2_gain,
    w_ffgate,
    w_ffup,
    w_down,
):
    parts = lax.axis_size("head")
    me = lax.axis_index("head")
    heads = decay_log.shape[0]
    query_width = conv_query.shape[1]
    value_width = conv_value.shape[1]
    dk = query_width // heads
    dv = value_width // heads
    margin = KW - 1
    gains = jnp.stack([norm1_gain, norm2_gain], axis=1)
    slabs_in = head_halves(
        [w_query, w_key, w_value, w_gate, w_rates, jnp.tile(gains, (1, parts))], parts
    )
    in_weight = whole_rows(swap_halves(slabs_in))
    rates_width = w_rates.shape[1] // parts
    mixed_width = 2 * query_width + value_width
    proj_width = mixed_width + value_width + rates_width
    gain_cols = in_weight[:, proj_width:].astype(jnp.float32)
    gain_one = gain_cols[:, 0]
    gain_two = gain_cols[:, 1]
    later = swap_halves(head_halves([w_out, w_ffgate, w_ffup, w_down], parts))
    ff_local = w_down.shape[1] // parts
    later_weight = whole_rows(later)
    out_weight = later_weight[:, :value_width]
    ff_weight = later_weight[:, value_width : value_width + 2 * ff_local]
    down_weight = later_weight[:, value_width + 2 * ff_local :]

    inputs_tok = tokens[0]
    own_count = inputs_tok.shape[0]
    piece_tok = lax.all_gather(inputs_tok, "head", axis=0, tiled=True)
    cot = lax.all_gather(cotangent[0], "head", axis=0, tiled=True)
    piece_tok, cot = lax.optimization_barrier((piece_tok, cot))
    residual = piece_tok.astype(jnp.float32)
    piece_rows = residual.shape[0]
    normed_one = rms_scale(residual, gain_one).astype(jnp.bfloat16)
    proj = mat_nn(normed_one, in_weight[:, :proj_width]).astype(jnp.bfloat16)
    joined = proj[:, :mixed_width]
    rates_here = proj[:, mixed_width + value_width :]
    rim_rows = passed_along(joined[piece_rows - margin :], "ctx", 1)
    padded = jnp.concatenate([rim_rows, joined], axis=0).astype(jnp.float32)
    conv_all = jnp.concatenate([conv_query, conv_key, conv_value], axis=1).astype(jnp.float32)
    mixed, conv_vjp = jax.vjp(short_conv, padded, conv_all)
    (log_decay, strength), rates_vjp = jax.vjp(
        decay_rates, rates_here.astype(jnp.float32), decay_log, decay_bias
    )
    value_first = 2 * query_width // dv
    chunk = min(CHUNK, piece_rows)
    chunks = piece_rows // chunk
    grid = (heads, chunks)
    log_decay = log_decay.reshape(heads, chunks, chunk, 1)
    strength = strength.reshape(heads, chunks, chunk, 1)
    mixed_specs = [
        columns(chunk, dk, 0),
        columns(chunk, dk, heads),
        columns(chunk, dv, value_first),
        heads_spec(chunk, 1),
        heads_spec(chunk, 1),
    ]
    square = heads_spec(chunk, chunk)
    state = heads_spec(dk, dv)
    rows_v = columns(chunk, dv, 0)
    rows_k = columns(chunk, dk, 0)
    inverse, local_out, effect, state_map, state_offset = per_head(
        forward_kernel,
        grid,
        mixed_specs,
        [
            (square, of_shape((heads, chunks, chunk, chunk))),
            (rows_v, of_shape((piece_rows, value_width))),
            (rows_k, of_shape((piece_rows, query_width))),
            (heads_spec(dk, dk), of_shape((heads, chunks, dk, dk))),
            (state, of_shape((heads, chunks, dk, dv))),
        ],
        (mixed, mixed, mixed, log_decay, strength),
        heads * 100 * piece_rows * chunk**2,
    )
    chunk_maps = [state_map[:, i] for i in range(chunks)]
    chunk_offsets = [state_offset[:, i] for i in range(chunks)]
    piece_map = chunk_maps[0]
    piece_offset = chunk_offsets[0]
    for i in range(1, chunks):
        piece_map = state_product(chunk_maps[i], piece_map)
        piece_offset = state_product(chunk_maps[i], piece_offset) + chunk_offsets[i]
    last_step = lax.axis_size("ctx") - 1
    start_state = jnp.zeros_like(piece_offset)
    for step in range(last_step):
        moved = piece_offset
        if step > 0:
            moved = moved + state_product(piece_map, start_state)
        start_state = passed_along(moved.astype(jnp.bfloat16), "ctx", 1).astype(jnp.float32)
    starts = [start_state]
    for i in range(1, chunks):
        starts.append(state_product(chunk_maps[i - 1], starts[-1]) + chunk_offsets[i - 1])
    start_states = jnp.stack(starts, axis=1)
    gain_row = out_gain.astype(jnp.float32)[None]
    gate_spec = columns(chunk, dv, mixed_width // dv)
    gain_spec = pl.BlockSpec((1, dv), lambda h, c: (0, h))
    gain_out = pl.BlockSpec((None, 1, dv), lambda h, c: (c, 0, h))
    gate_ins = [rows_v, rows_k, state, gate_spec, gain_spec]
    gate_args = (local_out, effect, start_states, proj, gain_row)
    (gated,) = per_head(
        gate_kernel,
        grid,
        gate_ins,
        [(rows_v, of_shape((piece_rows, value_width), jnp.bfloat16))],
        gate_args,
        heads * 12 * piece_rows * dk * dv,
    )
    middle = residual + head_sum(mat_nt(gated, out_weight))
    normed_two_f, norm_two_vjp = jax.vjp(rms_scale, middle, gain_two)
    normed_two = normed_two_f.astype(jnp.bfloat16)
    ff_both = mat_nn(normed_two, ff_weight)
    hidden_f, swiglu_vjp = jax.vjp(swiglu, ff_both[:, :ff_local], ff_both[:, ff_local:])
    hidden = hidden_f.astype(jnp.bfloat16)
    hidden_grad = mat_nn(cot, down_weight)
    gate_grad_f, up_grad_f = swiglu_vjp(hidden_grad)
    ff_grads = jnp.concatenate([gate_grad_f, up_grad_f], axis=1).astype(jnp.bfloat16)
    middle_part, gain_two_grad = norm_two_vjp(head_sum(mat_nt(ff_grads, ff_weight)))
    middle_grad = cot.astype(jnp.float32) + middle_part
    middle_grad_b = middle_grad.astype(jnp.bfloat16)
    gated_grad = mat_nn(middle_grad_b, out_weight).astype(jnp.bfloat16)
    middle_own = lax.dynamic_slice_in_dim(middle, me * own_count, own_count, 0)
    output_tok = (middle_own + own_rows_sum(mat_nt(hidden, down_weight))).astype(jnp.bfloat16)

    mixer_grad, gate_bf, out_gain_grad, reach = per_head(
        gate_back_kernel,
        grid,
        gate_ins + [rows_v],
        [
            (rows_v, of_shape((piece_rows, value_width))),
            (rows_v, of_shape((piece_rows, value_width), jnp.bfloat16)),
            (gain_out, of_shape((chunks, 1, value_width))),
            (state, of_shape((heads, chunks, dk, dv))),
        ],
        gate_args + (gated_grad,),
        heads * 24 * piece_rows * dk * dv,
    )
    chunk_reach = [reach[:, i] for i in range(chunks)]
    piece_reach = chunk_reach[chunks - 1]
    for i in range(chunks - 2, -1, -1):
        piece_reach = chunk_reach[i] + state_pull(chunk_maps[i], piece_reach)
    last_grad = jnp.zeros_like(piece_reach)
    for step in range(last_step):
        moved = piece_reach
        if step > 0:
            moved = moved + state_pull(piece_map, last_grad)
        last_grad = passed_along(moved.astype(jnp.bfloat16), "ctx", -1).astype(jnp.float32)
    lasts = [last_grad]
    for i in range(chunks - 1, 0, -1):
        lasts.insert(0, chunk_reach[i] + state_pull(chunk_maps[i], lasts[0]))
    last_grads = jnp.stack(lasts, axis=1)

    ff_products = jnp.concatenate(
        [
            mat_tn(middle_grad_b, gated).astype(jnp.bfloat16),
            mat_tn(normed_two, ff_grads).astype(jnp.bfloat16),
            mat_tn(cot, hidden).astype(jnp.bfloat16),
        ],
        axis=1,
    )
    last_grads, ff_products = lax.optimization_barrier((last_grads, ff_products))
    ff_sums = lax.psum_scatter(
        ff_products,
        ("ctx", "batch"),
        scatter_dimension=0,
        tiled=True,
    )

    query_g, key_g, value_g, decay_g, strength_g = per_head(
        backward_kernel,
        grid,
        mixed_specs + [square, state, rows_v, state],
        [
            (rows_k, of_shape((piece_rows, query_width))),
            (rows_k, of_shape((piece_rows, query_width))),
            (rows_v, of_shape((piece_rows, value_width))),
            (heads_spec(chunk, 1), of_shape((heads, chunks, chunk, 1))),
            (heads_spec(chunk, 1), of_shape((heads, chunks, chunk, 1))),
        ],
        (mixed, mixed, mixed, log_decay, strength, inverse, start_states, mixer_grad, last_grads),
        heads * 100 * piece_rows * chunk**2,
    )
    padded_grad, conv_grad = conv_vjp(jnp.concatenate([query_g, key_g, value_g], axis=1))
    rates_grad_f, decay_log_grad, decay_bias_grad = rates_vjp(
        (decay_g.reshape(heads, piece_rows, 1), strength_g.reshape(heads, piece_rows, 1))
    )
    back_rim = passed_along(padded_grad[:margin], "ctx", -1)
    own_rows = padded_grad[margin:]
    own_rows = jnp.concatenate(
        [own_rows[: piece_rows - margin], own_rows[piece_rows - margin :] + back_rim], axis=0
    ).astype(jnp.bfloat16)
    proj_grad = jnp.concatenate([own_rows, gate_bf, rates_grad_f.astype(jnp.bfloat16)], axis=1)
    proj_products = mat_tn(normed_one, proj_grad).astype(jnp.bfloat16)
    proj_products, ff_sums = lax.optimization_barrier((proj_products, ff_sums))
    ff_parts = split_columns(
        ff_sums.astype(jnp.float32), (value_width, ff_local, ff_local, ff_local)
    )
    proj_sums = lax.psum_scatter(
        proj_products,
        ("ctx", "batch"),
        scatter_dimension=0,
        tiled=True,
    ).astype(jnp.float32)
    proj_parts = split_columns(
        proj_sums, (query_width, query_width, value_width, value_width, rates_width)
    )
    own_grad = own_rows_sum(mat_nt(proj_grad, in_weight[:, :proj_width]))
    unused_rows, norm_one_vjp = jax.vjp(rms_scale, inputs_tok.astype(jnp.float32), gain_one)
    input_part, gain_one_grad = norm_one_vjp(own_grad)
    input_grad = lax.dynamic_slice_in_dim(middle_grad, me * own_count, own_count, 0) + input_part
    smalls = (
        conv_grad.reshape(-1),
        jnp.sum(out_gain_grad, axis=(0, 1)),
        head_sum(gain_one_grad, jnp.float32),
        gain_two_grad,
        decay_log_grad,
        decay_bias_grad,
    )
    summed = lax.psum(jnp.concatenate(smalls), ("ctx", "batch"))
    cuts = []
    first = 0
    for small in smalls:
        cuts.append(summed[first : first + small.shape[0]])
        first += small.shape[0]
    conv_sum = cuts[0].reshape(conv_grad.shape)
    share = norm1_gain.shape[0]
    place = (me * lax.axis_size("ctx") + lax.axis_index("ctx")) * lax.axis_size("batch")
    place = (place + lax.axis_index("batch")) * share
    return (
        output_tok[None],
        input_grad[None],
        lax.dynamic_slice_in_dim(cuts[2], place, share, 0),
        proj_parts[0],
        proj_parts[1],
        proj_parts[2],
        proj_parts[3],
        proj_parts[4],
        conv_sum[:, :query_width],
        conv_sum[:, query_width : 2 * query_width],
        conv_sum[:, 2 * query_width :],
        cuts[4],
        cuts[5],
        cuts[1],
        ff_parts[0],
        lax.dynamic_slice_in_dim(cuts[3], place, share, 0),
        ff_parts[1],
        ff_parts[2],
        ff_parts[3],
    )


def solution(mesh):
    placed = (
        P("batch", ("ctx", "head"), None),
        P("batch", ("ctx", "head"), None),
        P(("head", "ctx", "batch")),
        P(("head", "ctx", "batch"), None),
        P(("head", "ctx", "batch"), None),
        P(("head", "ctx", "batch"), None),
        P(("head", "ctx", "batch"), None),
        P(("head", "ctx", "batch"), None),
        P(None, "head"),
        P(None, "head"),
        P(None, "head"),
        P("head"),
        P("head"),
        P("head"),
        P(("head", "ctx", "batch"), None),
        P(("head", "ctx", "batch")),
        P(("head", "ctx", "batch"), None),
        P(("head", "ctx", "batch"), None),
        P(("head", "ctx", "batch"), None),
    )
    return jax.shard_map(
        body,
        mesh=mesh,
        in_specs=placed,
        out_specs=(
            P("batch", ("ctx", "head"), None),
            P("batch", ("ctx", "head"), None),
            P(("head", "ctx", "batch")),
            P(("ctx", "batch"), "head"),
            P(("ctx", "batch"), "head"),
            P(("ctx", "batch"), "head"),
            P(("ctx", "batch"), "head"),
            P(("ctx", "batch"), "head"),
            P(None, "head"),
            P(None, "head"),
            P(None, "head"),
            P("head"),
            P("head"),
            P("head"),
            P(("ctx", "batch"), "head"),
            P(("head", "ctx", "batch")),
            P(("ctx", "batch"), "head"),
            P(("ctx", "batch"), "head"),
            P(("ctx", "batch"), "head"),
        ),
        check_vma=False,
    )
```

profile of v0, /device:TPU:0, one launch (start us, length us, event | category | flops | bytes accessed | tf_op | source)
XLA Modules:
  0.0 518.8 jit_solution(7987486721188004493)
XLA Ops:
  11.2 11.4 %all_to_all.10 = bf16[2,32,3082]{2,1,0:T(8,128)(2,1)} all-to-all(bf16[2,32,3082]{2,1,0:T(8,128)(2,1)S(1)} %pad_maximum_fusion.6), channel_id=1, replica_groups=mesh['head'=2,'ctx'=4,'batch'=4] {'head'}, dimensions={0} | all-to-all | bytes 788992 | tf_op jit(solution)/shard_map/all_to_all | solution.py:313
  23.1 12.4 %all_to_all.11 = bf16[2,32,5248]{2,1,0:T(8,128)(2,1)} all-to-all(bf16[2,32,5248]{2,1,0:T(8,128)(2,1)S(1)} %pad_maximum_fusion.5), channel_id=1, replica_groups=mesh['head'=2,'ctx'=4,'batch'=4] {'head'}, dimensions={0} | all-to-all | bytes 1343488 | tf_op jit(solution)/shard_map/all_to_all | solution.py:313
  35.6 7.3 %all-gather.1 = bf16[1,256,1024]{2,1,0:T(8,128)(2,1)} all-gather(bf16[1,128,1024]{2,1,0:T(8,128)(2,1)S(1)} %copy-done.25), channel_id=3, replica_groups=mesh['head'=2,'ctx'=4,'batch'=4] {'head'}, dimensions={1}, use_global_device_ids=true | all-gather | bytes 786432 | tf_op jit(solution)/shard_map/all_gather | solution.py:401
  42.9 7.0 %all-gather = bf16[1,256,1024]{2,1,0:T(8,128)(2,1)S(1)} all-gather(bf16[1,128,1024]{2,1,0:T(8,128)(2,1)S(1)} %copy-done.16), channel_id=2, replica_groups=mesh['head'=2,'ctx'=4,'batch'=4] {'head'}, dimensions={1}, use_global_device_ids=true | all-gather | bytes 786432 | tf_op jit(solution)/shard_map/all_gather | solution.py:400
  50.2 36.0 %all-gather.5.cloned.1.call-done = bf16[2,512,3082]{2,1,0:T(8,128)(2,1)} async-done(((bf16[2,32,3082]{2,1,0:T(8,128)(2,1)}), bf16[2,512,3082]{2,1,0:T(8,128)(2,1)}) %all-gather.5.cloned.1.call-update) | async-done | bytes 6311952 | tf_op jit(solution)/shard_map/all_gather | solution.py:317
  87.5 4.9 fusion.4.gate_ref
  92.4 3.9 collective-permute-start
  101.6 39.0 %shard_map.330 = (f32[4,1,256,256]{3,2,1,0:T(8,128)}, f32[256,1024]{1,0:T(8,128)}, f32[256,512]{1,0:T(8,128)}, f32[4,1,128,128]{3,2,1,0:T(8,128)}, f32[4,1,128,256]{3,2,1,0:T(8,128)}) custom-call(f32[256,2048]{1,0:T(8,128)} %multiply_add_fusion.q_ref.k_ref.v_ref, f32[256,2048]{1,0:T(8,128)} %multiply_add_fusion.q_ref.k_ref.v_ref, ...), custom_call_target="tpu_custom_call" | custom-call | flops 6710886400 | bytes 6299648 | tf_op jit(solution)/shard_map/pallas_call | solution.py:218
  141.7 3.0 collective-permute-start.1
  144.7 12.0 %collective-permute-done.1 = bf16[4,128,256]{2,1,0:T(8,128)(2,1)S(1)} collective-permute-done((bf16[4,128,256]{2,1,0:T(8,128)(2,1)S(1)}, bf16[4,128,256]{2,1,0:T(8,128)(2,1)S(1)}, u32[]{:S(2)}, u32[]{:S(2)}) %collective-permute-start.1) | collective-permute-done | bytes 262176 | tf_op jit(solution)/shard_map/ppermute | solution.py:19
  158.2 7.3 %collective-permute-start.2 = (bf16[4,128,256]{2,1,0:T(8,128)(2,1)S(1)}, bf16[4,128,256]{2,1,0:T(8,128)(2,1)S(1)}, u32[]{:S(2)}, u32[]{:S(2)}) collective-permute-start(bf16[4,128,256]{2,1,0:T(8,128)(2,1)S(1)} %fusion.32), channel_id=1, source_target_pairs={{0,4},{4,8},{8,12},{1,5},{5,9},{9,13},{2,6},{6,10},{10,14},{3,7},{... | collective-permute-start | bytes 786440 | tf_op jit(solution)/shard_map/ppermute | solution.py:19
  165.5 11.9 %collective-permute-done.2 = bf16[4,128,256]{2,1,0:T(8,128)(2,1)S(1)} collective-permute-done((bf16[4,128,256]{2,1,0:T(8,128)(2,1)S(1)}, bf16[4,128,256]{2,1,0:T(8,128)(2,1)S(1)}, u32[]{:S(2)}, u32[]{:S(2)}) %collective-permute-start.2) | collective-permute-done | bytes 262176 | tf_op jit(solution)/shard_map/ppermute | solution.py:19
  177.8 6.4 %collective-permute-start.3 = (bf16[4,128,256]{2,1,0:T(8,128)(2,1)S(1)}, bf16[4,128,256]{2,1,0:T(8,128)(2,1)S(1)}, u32[]{:S(2)}, u32[]{:S(2)}) collective-permute-start(bf16[4,128,256]{2,1,0:T(8,128)(2,1)S(1)} %fusion.33), channel_id=1, source_target_pairs={{0,4},{4,8},{8,12},{1,5},{5,9},{9,13},{2,6},{6,10},{10,14},{3,7},{... | collective-permute-start | bytes 786440 | tf_op jit(solution)/shard_map/ppermute | solution.py:19
  184.8 4.8 collective-permute-done.3
  190.5 4.5 shard_map.331
  198.6 11.8 %collective-permute-done.4 = bf16[256,1024]{1,0:T(8,128)(2,1)S(1)} collective-permute-done((bf16[256,1024]{1,0:T(8,128)(2,1)S(1)}, bf16[256,1024]{1,0:T(8,128)(2,1)S(1)}, u32[]{:S(2)}, u32[]{:S(2)}) %collective-permute-start.4) | collective-permute-done | bytes 524320 | tf_op jit(solution)/shard_map/ppermute | solution.py:325
  210.8 4.5 fusion.9
  220.6 4.3 convolution_convert_fusion.1
  224.9 7.3 %collective-permute-done.6 = bf16[256,1024]{1,0:T(8,128)(2,1)S(1)} collective-permute-done((bf16[256,1024]{1,0:T(8,128)(2,1)S(1)}, bf16[256,1024]{1,0:T(8,128)(2,1)S(1)}, u32[]{:S(2)}, u32[]{:S(2)}) %collective-permute-start.6) | collective-permute-done | bytes 524320 | tf_op jit(solution)/shard_map/ppermute | solution.py:325
  235.6 6.1 %shard_map.332 = (f32[256,1024]{1,0:T(8,128)}, bf16[256,1024]{1,0:T(8,128)(2,1)}, f32[1,1,1024]{2,1,0:T(1,128)}, f32[4,1,128,256]{3,2,1,0:T(8,128)}) custom-call(f32[256,1024]{1,0:T(8,128)} %get-tuple-element.40.o_ref, f32[256,512]{1,0:T(8,128)} %get-tuple-element.41.e_ref, f32[4,1,128,256]{3,2,1,0:T(8,128)} %bitcast_convert_fusion.3.i_ref, ...), custom_call_target="tpu_custom_call" | custom-call | flops 805306368 | bytes 4202496 | tf_op jit(solution)/shard_map/pallas_call | solution.py:218
  244.1 4.0 convolution_convert_fusion.2
  248.1 3.4 collective-permute-done.7
  256.3 3.9 copy.122
  265.2 9.7 %pad_maximum_fusion = bf16[1024,5248]{1,0:T(8,128)(2,1)} fusion(bf16[1024,1408]{1,0:T(8,128)(2,1)} %convolution_convert_fusion.2, bf16[1024,2816]{1,0:T(8,128)(2,1)} %convolution_convert_fusion.1, bf16[1024,1024]{1,0:T(8,128)(2,1)} %copy.122), kind=kLoop, calls=%fused_computation | loop fusion | flops 32243712 | bytes 21495808 | tf_op jit(solution)/shard_map/concatenate | solution.py:523
  275.9 27.6 %shard_map.333 = (f32[256,512]{1,0:T(8,128)}, f32[256,512]{1,0:T(8,128)}, f32[256,1024]{1,0:T(8,128)}, f32[4,1,256,1]{3,2,1,0:T(8,128)}, f32[4,1,256,1]{3,2,1,0:T(8,128)}) custom-call(f32[256,2048]{1,0:T(8,128)} %multiply_add_fusion.q_ref.k_ref.v_ref, f32[256,2048]{1,0:T(8,128)} %multiply_add_fusion.q_ref.k_ref.v_ref, ...), custom_call_target="tpu_custom_call" | custom-call | flops 6710886400 | bytes 9445376 | tf_op jit(solution)/shard_map/pallas_call | solution.py:218
  319.1 4.6 convolution_convert_fusion
  323.7 76.8 %reduce-scatter.5.cloned.1.call-done = bf16[64,5248]{1,0:T(8,128)(2,1)} async-done(((bf16[1024,5248]{1,0:T(8,128)(2,1)}), bf16[64,5248]{1,0:T(8,128)(2,1)}) %reduce-scatter.5.cloned.1.call-update) | async-done | bytes 671760 | tf_op jit(solution)/shard_map/reduce_scatter | solution.py:532
  400.5 8.9 %copy.133 = bf16[1024,3080]{1,0:T(8,128)(2,1)} copy(bf16[1024,3080]{0,1:T(8,128)(2,1)} %convolution_convert_fusion) | data formatting | bytes 12615680
  416.2 6.0 %collective-permute-done.5 = bf16[128,1024]{1,0:T(8,128)(2,1)S(1)} collective-permute-done((bf16[128,1024]{1,0:T(8,128)(2,1)S(1)}, bf16[128,1024]{1,0:T(8,128)(2,1)S(1)}, u32[]{:S(2)}, u32[]{:S(2)}) %collective-permute-start.5) | collective-permute-done | bytes 262176 | tf_op jit(solution)/shard_map/ppermute | solution.py:347
  424.3 5.5 %fusion = f32[256,1024]{1,0:T(8,128)S(1)} fusion(bf16[1024,3082]{1,0:T(8,128)(2,1)} %bitcast.138, bf16[256,8]{1,0:T(8,128)(2,1)S(1)} %copy.125, bf16[256,1024]{1,0:T(8,128)(2,1)} %get-tuple-element.52, bf16[3,2048]{1,0:T(4,128)(2,1)S(1)} %fusion.57, bf16[253,2048]{1,0:T(8,128)(2,1)S(1)} %copy-done.21), kind=kOutput, calls=%fused_computation.2 | convolution fusion | flops 1621114880 | bytes 8937472 | tf_op jit(solution)/shard_map/dot_general | solution.py:251
  431.5 5.3 %collective-permute-done.11 = bf16[128,1024]{1,0:T(8,128)(2,1)S(1)} collective-permute-done((bf16[128,1024]{1,0:T(8,128)(2,1)S(1)}, bf16[128,1024]{1,0:T(8,128)(2,1)S(1)}, u32[]{:S(2)}, u32[]{:S(2)}) %collective-permute-start.11) | collective-permute-done | bytes 262176 | tf_op jit(solution)/shard_map/ppermute | solution.py:347
  440.8 60.4 %psum.7 = f32[11272]{0:T(1024)S(1)} all-reduce(f32[11272]{0:T(1024)S(1)} %concatenate.49), channel_id=1, replica_groups=mesh['head'=2,'ctx'=4,'batch'=4] {'ctx','batch'}, use_global_device_ids=true, to_apply=%region_13.14 | all-reduce | flops 11272 | bytes 90176 | tf_op jit(solution)/shard_map/psum | solution.py:589
  (208 shorter events, 81.6 us)
Async XLA Ops:
  7.2 15.5 %copy-start.29 = (bf16[32,2048]{1,0:T(8,128)(2,1)S(1)}, bf16[32,2048]{1,0:T(8,128)(2,1)}, u32[]{:S(2)}) copy-start(bf16[32,2048]{1,0:T(8,128)(2,1)} %param.33) | copy-start | bytes 393220
  7.2 15.5 %copy-start.26 = (bf16[32,2816]{1,0:T(8,128)(2,1)S(1)}, bf16[32,2816]{1,0:T(8,128)(2,1)}, u32[]{:S(2)}) copy-start(bf16[32,2816]{1,0:T(8,128)(2,1)} %param.35) | copy-start | bytes 540676
  7.2 79.0 %all-gather.5.cloned.1.call-start = ((), (), s32[]{:S(2)}) async-start(), calls=%async_computation.4 | async-start | bytes 6963200 | tf_op jit(solution)/shard_map/all_gather | solution.py:317
  9.1 13.6 %copy-start.27 = (bf16[32,2816]{1,0:T(8,128)(2,1)S(1)}, bf16[32,2816]{1,0:T(8,128)(2,1)}, u32[]{:S(2)}) copy-start(bf16[32,2816]{1,0:T(8,128)(2,1)} %param.36) | copy-start | bytes 540676
  10.0 12.8 %copy-start.28 = (bf16[32,2816]{1,0:T(8,128)(2,1)S(1)}, bf16[32,2816]{1,0:T(8,128)(2,1)}, u32[]{:S(2)}) copy-start(bf16[32,2816]{1,0:T(8,128)(2,1)} %param.37) | copy-start | bytes 540676
  22.7 172.3 %all-gather.7.cloned.1.call-start = ((), (), s32[]{:S(2)}) async-start(), calls=%async_computation.5 | async-start | bytes 11419648 | tf_op jit(solution)/shard_map/all_gather | solution.py:317
  22.9 20.0 %copy-start.16 = (bf16[1,128,1024]{2,1,0:T(8,128)(2,1)S(1)}, bf16[1,128,1024]{2,1,0:T(8,128)(2,1)}, u32[]{:S(2)}) copy-start(bf16[1,128,1024]{2,1,0:T(8,128)(2,1)} %param.19) | copy-start | bytes 786436
  23.0 27.1 %copy-start.38 = (f32[4]{0:T(128)S(1)}, f32[4]{0:T(128)}, u32[]{:S(2)}) copy-start(f32[4]{0:T(128)} %param.30) | copy-start | bytes 52
  23.0 27.1 %copy-start.30 = (bf16[4,1024]{1,0:T(4,128)(2,1)S(1)}, bf16[4,1024]{1,0:T(4,128)(2,1)}, u32[]{:S(2)}) copy-start(bf16[4,1024]{1,0:T(4,128)(2,1)} %param.29) | copy-start | bytes 24580
  23.0 27.1 %copy-start.32 = (bf16[4,512]{1,0:T(4,128)(2,1)S(1)}, bf16[4,512]{1,0:T(4,128)(2,1)}, u32[]{:S(2)}) copy-start(bf16[4,512]{1,0:T(4,128)(2,1)} %param.28) | copy-start | bytes 12292
  23.0 27.1 %copy-start.33 = (bf16[4,512]{1,0:T(4,128)(2,1)S(1)}, bf16[4,512]{1,0:T(4,128)(2,1)}, u32[]{:S(2)}) copy-start(bf16[4,512]{1,0:T(4,128)(2,1)} %param.27) | copy-start | bytes 12292
  35.5 365.0 %reduce-scatter.5.cloned.1.call-start = ((), (), s32[]{:S(2)}) async-start(), calls=%async_computation.6 | async-start | bytes 11419648 | tf_op jit(solution)/shard_map/reduce_scatter | solution.py:532
  49.9 42.4 %copy-start.10 = (bf16[1,256,1024]{2,1,0:T(8,128)(2,1)}, bf16[1,256,1024]{2,1,0:T(8,128)(2,1)S(1)}, u32[]{:S(2)}) copy-start(bf16[1,256,1024]{2,1,0:T(8,128)(2,1)S(1)} %all-gather) | copy-start | bytes 1572868
  92.4 6.7 %collective-permute-start = (bf16[3,2048]{1,0:T(4,128)(2,1)S(1)}, bf16[3,2048]{1,0:T(4,128)(2,1)S(1)}, u32[]{:S(2)}, u32[]{:S(2)}) collective-permute-start(bf16[3,2048]{1,0:T(4,128)(2,1)S(1)} %slice.261), channel_id=1, source_target_pairs={{0,4},{4,8},{8,12},{1,5},{5,9},{9,13},{2,6},{6,10},{10,14},{3,7},{... | collective-permute-start | bytes 36872 | tf_op jit(solution)/shard_map/ppermute | solution.py:19
  140.6 36.9 %copy-start.14 = (f32[4,1,128,256]{3,2,1,0:T(8,128)S(1)}, f32[4,1,128,256]{3,2,1,0:T(8,128)}, u32[]{:S(2)}) copy-start(f32[4,1,128,256]{3,2,1,0:T(8,128)} %get-tuple-element.42) | copy-start | bytes 1572868
  140.6 36.9 %copy-start.15 = (f32[4,1,128,128]{3,2,1,0:T(8,128)S(1)}, f32[4,1,128,128]{3,2,1,0:T(8,128)}, u32[]{:S(2)}) copy-start(f32[4,1,128,128]{3,2,1,0:T(8,128)} %get-tuple-element.43) | copy-start | bytes 786436
  140.6 43.6 %copy-start.35 = (bf16[1024]{0:T(1024)(128)(2,1)S(1)}, bf16[1024]{0:T(1024)(128)(2,1)}, u32[]{:S(2)}) copy-start(bf16[1024]{0:T(1024)(128)(2,1)} %param.32) | copy-start | bytes 6148
  141.7 15.0 %collective-permute-start.1 = (bf16[4,128,256]{2,1,0:T(8,128)(2,1)S(1)}, bf16[4,128,256]{2,1,0:T(8,128)(2,1)S(1)}, u32[]{:S(2)}, u32[]{:S(2)}) collective-permute-start(bf16[4,128,256]{2,1,0:T(8,128)(2,1)S(1)} %bitcast_convert_fusion.1), channel_id=1, source_target_pairs={{0,4},{4,8},{8,12},{1,5},{5,9},{9,13},{2,6},{6,10},{10,14},{3,7},{... | collective-permute-start | bytes 786440 | tf_op jit(solution)/shard_map/ppermute | solution.py:19
  158.2 19.3 %collective-permute-start.2 = (bf16[4,128,256]{2,1,0:T(8,128)(2,1)S(1)}, bf16[4,128,256]{2,1,0:T(8,128)(2,1)S(1)}, u32[]{:S(2)}, u32[]{:S(2)}) collective-permute-start(bf16[4,128,256]{2,1,0:T(8,128)(2,1)S(1)} %fusion.32), channel_id=1, source_target_pairs={{0,4},{4,8},{8,12},{1,5},{5,9},{9,13},{2,6},{6,10},{10,14},{3,7},{... | collective-permute-start | bytes 786440 | tf_op jit(solution)/shard_map/ppermute | solution.py:19
  177.8 11.8 %collective-permute-start.3 = (bf16[4,128,256]{2,1,0:T(8,128)(2,1)S(1)}, bf16[4,128,256]{2,1,0:T(8,128)(2,1)S(1)}, u32[]{:S(2)}, u32[]{:S(2)}) collective-permute-start(bf16[4,128,256]{2,1,0:T(8,128)(2,1)S(1)} %fusion.33), channel_id=1, source_target_pairs={{0,4},{4,8},{8,12},{1,5},{5,9},{9,13},{2,6},{6,10},{10,14},{3,7},{... | collective-permute-start | bytes 786440 | tf_op jit(solution)/shard_map/ppermute | solution.py:19
  194.9 15.5 %copy-start.11 = (bf16[1,256,1024]{2,1,0:T(8,128)(2,1)S(1)}, bf16[1,256,1024]{2,1,0:T(8,128)(2,1)}, u32[]{:S(2)}) copy-start(bf16[1,256,1024]{2,1,0:T(8,128)(2,1)} %copy-done.10) | copy-start | bytes 1572868
  197.5 12.9 %collective-permute-start.4 = (bf16[256,1024]{1,0:T(8,128)(2,1)S(1)}, bf16[256,1024]{1,0:T(8,128)(2,1)S(1)}, u32[]{:S(2)}, u32[]{:S(2)}) collective-permute-start(bf16[256,1024]{1,0:T(8,128)(2,1)S(1)} %fusion.23), channel_id=1, source_target_pairs={{0,16},{16,0},{1,17},{17,1},{2,18},{18,2},{3,19},{19,3},{4,20},{20... | collective-permute-start | bytes 1572872 | tf_op jit(solution)/shard_map/ppermute | solution.py:325
  220.2 12.1 %collective-permute-start.6 = (bf16[256,1024]{1,0:T(8,128)(2,1)S(1)}, bf16[256,1024]{1,0:T(8,128)(2,1)S(1)}, u32[]{:S(2)}, u32[]{:S(2)}) collective-permute-start(bf16[256,1024]{1,0:T(8,128)(2,1)S(1)} %fusion.29), channel_id=1, source_target_pairs={{0,16},{16,0},{1,17},{17,1},{2,18},{18,2},{3,19},{19,3},{4,20},{20... | collective-permute-start | bytes 1572872 | tf_op jit(solution)/shard_map/ppermute | solution.py:325
  242.8 8.7 %collective-permute-start.7 = (bf16[4,128,256]{2,1,0:T(8,128)(2,1)S(1)}, bf16[4,128,256]{2,1,0:T(8,128)(2,1)S(1)}, u32[]{:S(2)}, u32[]{:S(2)}) collective-permute-start(bf16[4,128,256]{2,1,0:T(8,128)(2,1)S(1)} %bitcast_convert_fusion), channel_id=1, source_target_pairs={{4,0},{8,4},{12,8},{5,1},{9,5},{13,9},{6,2},{10,6},{14,10},{7,3},{... | collective-permute-start | bytes 786440 | tf_op jit(solution)/shard_map/ppermute | solution.py:19
  252.7 9.0 %collective-permute-start.8 = (bf16[4,128,256]{2,1,0:T(8,128)(2,1)}, bf16[4,128,256]{2,1,0:T(8,128)(2,1)}, u32[]{:S(2)}, u32[]{:S(2)}) collective-permute-start(bf16[4,128,256]{2,1,0:T(8,128)(2,1)} %fusion.34), channel_id=1, source_target_pairs={{4,0},{8,4},{12,8},{5,1},{9,5},{13,9},{6,2},{10,6},{14,10},{7,3},{... | collective-permute-start | bytes 786440 | tf_op jit(solution)/shard_map/ppermute | solution.py:19
  263.9 11.0 %collective-permute-start.9 = (bf16[4,128,256]{2,1,0:T(8,128)(2,1)}, bf16[4,128,256]{2,1,0:T(8,128)(2,1)S(1)}, u32[]{:S(2)}, u32[]{:S(2)}) collective-permute-start(bf16[4,128,256]{2,1,0:T(8,128)(2,1)} %fusion.35), channel_id=1, source_target_pairs={{4,0},{8,4},{12,8},{5,1},{9,5},{13,9},{6,2},{10,6},{14,10},{7,3},{... | collective-permute-start | bytes 786440 | tf_op jit(solution)/shard_map/ppermute | solution.py:19
  275.8 230.7 %reduce-scatter.7.cloned.1.call-start = ((), (), s32[]{:S(2)}) async-start(), calls=%async_computation.7 | async-start | bytes 6963200
  310.1 7.5 %collective-permute-start.10 = (f32[3,2048]{1,0:T(4,128)S(1)}, f32[3,2048]{1,0:T(4,128)S(1)}, u32[]{:S(2)}, u32[]{:S(2)}) collective-permute-start(f32[3,2048]{1,0:T(4,128)S(1)} %pad_add_fusion.1), channel_id=1, source_target_pairs={{4,0},{8,4},{12,8},{5,1},{9,5},{13,9},{6,2},{10,6},{14,10},{7,3},{... | collective-permute-start | bytes 73736 | tf_op jit(solution)/shard_map/ppermute | solution.py:19
  414.5 7.7 %collective-permute-start.5 = (bf16[128,1024]{1,0:T(8,128)(2,1)S(1)}, bf16[128,1024]{1,0:T(8,128)(2,1)S(1)}, u32[]{:S(2)}, u32[]{:S(2)}) collective-permute-start(bf16[128,1024]{1,0:T(8,128)(2,1)S(1)} %dynamic-slice_convert_fusion.1), channel_id=1, source_target_pairs={{0,16},{16,0},{1,17},{17,1},{2,18},{18,2},{3,19},{19,3},{4,20},{20... | collective-permute-start | bytes 786440 | tf_op jit(solution)/shard_map/ppermute | solution.py:347
  429.9 74.9 %copy-start.18 = (bf16[64,5248]{1,0:T(8,128)(2,1)S(1)}, bf16[64,5248]{1,0:T(8,128)(2,1)}, u32[]{:S(2)}) copy-start(bf16[64,5248]{1,0:T(8,128)(2,1)} %reduce-scatter.5.cloned.1.call-done) | copy-start | bytes 2015236
  429.9 6.9 %collective-permute-start.11 = (bf16[128,1024]{1,0:T(8,128)(2,1)S(1)}, bf16[128,1024]{1,0:T(8,128)(2,1)S(1)}, u32[]{:S(2)}, u32[]{:S(2)}) collective-permute-start(bf16[128,1024]{1,0:T(8,128)(2,1)S(1)} %dynamic-slice_convert_fusion), channel_id=1, source_target_pairs={{0,16},{16,0},{1,17},{17,1},{2,18},{18,2},{3,19},{19,3},{4,20},{20... | collective-permute-start | bytes 786440 | tf_op jit(solution)/shard_map/ppermute | solution.py:347
  437.1 3.7 collective-permute-start.12
  (24 other events, 124.5 us)
Sparse Core Ops, SparseCore 0:
  22.8 63.3 all-gather.4
  88.5 91.9 all-gather.6
  275.9 124.5 reduce-scatter.4
  409.6 87.1 reduce-scatter.6
where the time goes:
time: 523 us; the launch traced here: 519 us
  waiting for transfers between devices  178 us (34%)
  blocking collectives  98.6 us (19%)
  Pallas kernels  77.3 us (15%)
  matrix products  46 us (9%)
  local copies, waits for them, and re-layouts  40.1 us (8%)
  starting transfers between devices  32.5 us (6%)
  other arithmetic  31.3 us (6%)
  between operations  14.9 us (3%)
    pallas_call x4, Pallas kernels, per_head(): pl.pallas_call(kernel, grid=grid, in_specs=ins, out_specs=[spec for spec,...  77.3 us
    reduce_scatter x1, waiting for transfers between devices, body(): lax.psum_scatter(ff_products, ('ctx', 'batch'), scatter_dimension=0, tile...  76.8 us
    psum x1, blocking collectives, body(): summed = lax.psum(jnp.concatenate(smalls), ('ctx', 'batch'))  60.4 us
    all_gather x2, waiting for transfers between devices, whole_rows(): full = lax.all_gather(slabs, ('ctx', 'batch'), axis=1, tiled=True)  36 us
    ppermute x8, waiting for transfers between devices, passed_along(): return lax.ppermute(block, axis, route)  33.6 us
    ppermute x8, starting transfers between devices, passed_along(): return lax.ppermute(block, axis, route)  26.2 us
    all_to_all x2, blocking collectives, swap_halves(): lax.all_to_all(slabs, 'head', split_axis=0, concat_axis=0, tiled=True)  23.8 us
    unnamed x88, local copies, waits for them, and re-layouts  22.3 us
  transfers between devices with their start and end apart: 17, of which 13 were waited for; matrix products, arithmetic and copies ran while one was open for 14% of the time, Pallas kernels for 14%

commit v1 on v0

--- a/solution.py
+++ b/solution.py
@@ -1,3 +1,4 @@
+import functools
 import math
 
 import jax
@@ -19,14 +20,27 @@
     return lax.ppermute(block, axis, route)
 
 
-def product(first, second, first_dim, second_dim):
+def halves(matrix):
+    high = matrix.astype(jnp.bfloat16)
+    return high, (matrix - high.astype(jnp.float32)).astype(jnp.bfloat16)
+
+
+def one_pass(first, second, first_dim, second_dim):
     return lax.dot_general(
         first,
         second,
         (((first_dim,), (second_dim,)), ((), ())),
-        precision=highest_precision,
         preferred_element_type=jnp.float32,
     )
+
+
+def product(first, second, first_dim, second_dim):
+    first_high, first_low = halves(first)
+    second_high, second_low = halves(second)
+    small = one_pass(first_low, second_high, first_dim, second_dim) + one_pass(
+        first_high, second_low, first_dim, second_dim
+    )
+    return small + one_pass(first_high, second_high, first_dim, second_dim)
 
 
 @jax.custom_vjp
@@ -310,6 +324,12 @@
 
 
 def swap_halves(slabs):
+    if slabs.shape[0] == 2:
+        me = lax.axis_index("head")
+        sent = lax.dynamic_index_in_dim(slabs, 1 - me, 0, keepdims=False)
+        kept = lax.dynamic_index_in_dim(slabs, me, 0, keepdims=False)
+        moved = lax.ppermute(sent, "head", [(0, 1), (1, 0)])
+        return jnp.where(me == 0, jnp.stack([kept, moved]), jnp.stack([moved, kept]))
     return lax.all_to_all(slabs, "head", split_axis=0, concat_axis=0, tiled=True)
 
 
@@ -346,6 +366,492 @@
         route = [(i, (i + shift) % parts) for i in range(parts)]
         total = total + lax.ppermute(sent, "head", route).astype(jnp.float32)
     return total
+
+
+MESH_ID = pl.DeviceIdType.MESH
+PAIR = 2
+
+
+def staged(rows):
+    parts = lax.axis_size("ctx") * lax.axis_size("batch")
+    return lax.axis_size("batch") == 2 * PAIR and rows % parts == 0 and (rows // parts) % 16 == 0
+
+
+def places():
+    c = lax.axis_index("ctx")
+    b = lax.axis_index("batch")
+    k = lax.rem(b, PAIR)
+    x = lax.div(b, PAIR)
+    return c, x, k, x * PAIR + (1 - k), (1 - x) * PAIR + k
+
+
+def greet(n, partner, across, c, facing=None):
+    barrier = pltpu.get_barrier_semaphore()
+    count = n + 1
+    if facing is not None:
+        pl.semaphore_signal(barrier, inc=1, device_id={"head": facing}, device_id_type=MESH_ID)
+        count += 1
+    for shift in range(1, n):
+        pl.semaphore_signal(
+            barrier, inc=1, device_id={"ctx": lax.rem(c + shift, n)}, device_id_type=MESH_ID
+        )
+    for other in (partner, across):
+        pl.semaphore_signal(barrier, inc=1, device_id={"batch": other}, device_id_type=MESH_ID)
+    pl.semaphore_wait(barrier, count)
+
+
+def scatter_kernel(
+    n, steps, widths, a_ref, sm_ref, *refs
+):
+    outs = refs[: len(widths)]
+    (
+        sm_out, from_pair, paired, from_across, held, from_left, from_right, acc,
+        sm_in, sm_sent, sm_all,
+        pair_send, pair_recv, cross_send, cross_recv, line_send, left_recv, right_recv,
+        sm_send, sm_recv, all_send, all_recv,
+    ) = refs[len(widths) :]
+    c, x, k, partner, across = places()
+    right = jnp.minimum(c + 1, n - 1)
+    left = jnp.maximum(c - 1, 0)
+    greet(n, partner, across, c)
+
+    def to_pair(q):
+        return pltpu.make_async_remote_copy(
+            a_ref.at[:, :, 1 - k, q], from_pair.at[q], pair_send.at[q], pair_recv.at[q],
+            device_id={"batch": partner}, device_id_type=MESH_ID,
+        )
+
+    def to_across(q):
+        return pltpu.make_async_remote_copy(
+            paired.at[q, 1 - x], from_across.at[q], cross_send.at[q], cross_recv.at[q],
+            device_id={"batch": across}, device_id_type=MESH_ID,
+        )
+
+    def to_right(q, at):
+        return pltpu.make_async_remote_copy(
+            held.at[q, at], from_left.at[q, at], line_send.at[q, at], left_recv.at[q, at],
+            device_id={"ctx": right}, device_id_type=MESH_ID,
+        )
+
+    def to_left(q, at):
+        return pltpu.make_async_remote_copy(
+            held.at[q, at], from_right.at[q, at], line_send.at[q, at], right_recv.at[q, at],
+            device_id={"ctx": left}, device_id_type=MESH_ID,
+        )
+
+    def small(source, stage, other):
+        return pltpu.make_async_remote_copy(
+            source, sm_in.at[stage], sm_send.at[stage], sm_recv.at[stage],
+            device_id={"batch": other}, device_id_type=MESH_ID,
+        )
+
+    def small_all(shift):
+        peer = lax.rem(c + shift, n)
+        return pltpu.make_async_remote_copy(
+            sm_sent.at[1], sm_all.at[c], all_send.at[shift], all_recv.at[n - shift],
+            device_id={"ctx": peer}, device_id_type=MESH_ID,
+        )
+
+    def small_from(shift):
+        peer = lax.rem(c + shift, n)
+        return pltpu.make_async_remote_copy(
+            sm_sent.at[1], sm_all.at[peer], all_send.at[shift], all_recv.at[shift],
+            device_id={"ctx": peer}, device_id_type=MESH_ID,
+        )
+
+    def begin(q, carry):
+        to_pair(q).start()
+        return carry
+
+    lax.fori_loop(0, steps, begin, 0)
+    first_small = small(sm_ref, 0, partner)
+    first_small.start()
+
+    def pair_up(q, carry):
+        to_pair(q).wait_recv()
+
+        def add(at, inner):
+            for side in range(2):
+                total = a_ref[at, side, k, q].astype(jnp.float32) + from_pair[
+                    q, at, side
+                ].astype(jnp.float32)
+                paired[q, side, at] = total.astype(jnp.bfloat16)
+            return inner
+
+        lax.fori_loop(0, n, add, 0)
+        to_across(q).start()
+        return carry
+
+    lax.fori_loop(0, steps, pair_up, 0)
+    first_small.wait()
+    sm_sent[0] = sm_ref[...] + sm_in[0]
+    second_small = small(sm_sent.at[0], 1, across)
+    second_small.start()
+
+    def cross_up(q):
+        to_across(q).wait_recv()
+
+        def add(at, inner):
+            total = paired[q, x, at].astype(jnp.float32) + from_across[q, at].astype(jnp.float32)
+            held[q, at] = total.astype(jnp.bfloat16)
+            return inner
+
+        lax.fori_loop(0, n, add, 0)
+
+        @pl.when(c == 0)
+        def _():
+            for at in range(n - 1, 0, -1):
+                to_right(q, at).start()
+
+        @pl.when(c == n - 1)
+        def _():
+            for at in range(n - 1):
+                to_left(q, at).start()
+
+    def relay(q):
+        for near in range(n - 2):
+            far = n - 1 - near
+
+            @pl.when((c > 0) & (c < far))
+            def _():
+                to_right(q, far).wait_recv()
+                total = held[q, far].astype(jnp.float32) + from_left[q, far].astype(jnp.float32)
+                held[q, far] = total.astype(jnp.bfloat16)
+                to_right(q, far).start()
+
+            @pl.when((c < n - 1) & (c > near))
+            def _():
+                to_left(q, near).wait_recv()
+                total = held[q, near].astype(jnp.float32) + from_right[q, near].astype(
+                    jnp.float32
+                )
+                held[q, near] = total.astype(jnp.bfloat16)
+                to_left(q, near).start()
+
+        acc[...] = paired[q, x, c].astype(jnp.float32) + from_across[q, c].astype(jnp.float32)
+
+        @pl.when(c > 0)
+        def _():
+            to_right(q, c).wait_recv()
+            acc[...] += from_left[q, c].astype(jnp.float32)
+
+        @pl.when(c < n - 1)
+        def _():
+            to_left(q, c).wait_recv()
+            acc[...] += from_right[q, c].astype(jnp.float32)
+
+        first = 0
+        for out, width in zip(outs, widths):
+            out[q] = acc[:, first : first + width]
+            first += width
+
+    cross_up(0)
+    second_small.wait()
+    sm_sent[1] = sm_sent[0] + sm_in[1]
+    for shift in range(1, n):
+        small_all(shift).start()
+
+    def middle(q, carry):
+        cross_up(q + 1)
+        relay(q)
+        return carry
+
+    lax.fori_loop(0, steps - 1, middle, 0)
+    relay(steps - 1)
+    sm_all[c] = sm_sent[1]
+    for shift in range(1, n):
+        small_from(shift).wait_recv()
+        small_all(shift).wait_send()
+    total = sm_all[0]
+    for at in range(1, n):
+        total = total + sm_all[at]
+    sm_out[...] = total
+
+    def drain(q, carry):
+        to_pair(q).wait_send()
+        to_across(q).wait_send()
+
+        def line(at, inner):
+            @pl.when(at > c)
+            def _():
+                to_right(q, at).wait_send()
+
+            @pl.when(at < c)
+            def _():
+                to_left(q, at).wait_send()
+
+            return inner
+
+        lax.fori_loop(0, n, line, 0)
+        return carry
+
+    lax.fori_loop(0, steps, drain, 0)
+
+
+def scatter_sum(products, smalls, widths):
+    n = lax.axis_size("ctx")
+    parts = n * lax.axis_size("batch")
+    rows = products.shape[0] // parts
+    cols = products.shape[1]
+    steps = rows // 16
+    blocks = products.reshape(n, 2, 2, steps, 16, cols)
+    count = smalls.shape[0]
+    lanes = pl.cdiv(count, 1024) * 8
+    flat = jnp.pad(smalls, (0, lanes * 128 - count)).reshape(lanes, 128)
+    vmem = pl.BlockSpec(memory_space=pltpu.VMEM)
+    half = jnp.bfloat16
+    dma = pltpu.SemaphoreType.DMA
+    results = pl.pallas_call(
+        functools.partial(scatter_kernel, n, steps, widths),
+        in_specs=[vmem, vmem],
+        out_specs=[vmem] * (len(widths) + 1),
+        out_shape=[of_shape((steps, 16, width)) for width in widths] + [of_shape(flat.shape)],
+        scratch_shapes=[
+            pltpu.VMEM((steps, n, 2, 16, cols), half),
+            pltpu.VMEM((steps, 2, n, 16, cols), half),
+            pltpu.VMEM((steps, n, 16, cols), half),
+            pltpu.VMEM((steps, n, 16, cols), half),
+            pltpu.VMEM((steps, n, 16, cols), half),
+            pltpu.VMEM((steps, n, 16, cols), half),
+            pltpu.VMEM((16, cols), jnp.float32),
+            pltpu.VMEM((2,) + flat.shape, jnp.float32),
+            pltpu.VMEM((2,) + flat.shape, jnp.float32),
+            pltpu.VMEM((n,) + flat.shape, jnp.float32),
+            dma((steps,)), dma((steps,)), dma((steps,)), dma((steps,)),
+            dma((steps, n)), dma((steps, n)), dma((steps, n)),
+            dma((2,)), dma((2,)), dma((n,)), dma((n,)),
+        ],
+        compiler_params=pltpu.CompilerParams(collective_id=0, has_side_effects=True),
+        cost_estimate=pl.CostEstimate(
+            flops=0, bytes_accessed=4 * products.size * 2, transcendentals=0
+        ),
+    )(blocks, flat)
+    sums = [result.reshape(rows, width) for result, width in zip(results, widths)]
+    return sums, results[-1].reshape(-1)[:count]
+
+
+def gather_kernel(n, slab_ref, tok_ref, cot_ref, *refs):
+    (
+        out, tok_out, cot_out,
+        own_sem, side_send, side_recv, line_send, line_recv,
+        cross_send, cross_recv, pair_send, pair_recv,
+    ) = refs
+    c, x, k, partner, across = places()
+    me = lax.axis_index("head")
+    other = 1 - me
+    right = jnp.minimum(c + 1, n - 1)
+    left = jnp.maximum(c - 1, 0)
+    greet(n, partner, across, c, other)
+
+    def copy(source, target, send, recv, axis, to):
+        return pltpu.make_async_remote_copy(
+            source, target, send, recv, device_id={axis: to}, device_id_type=MESH_ID
+        )
+
+    def piece(j, at, side, core):
+        return out.at[me if j == 0 else other, at, side, core]
+
+    def to_line(j, at, to, source=None):
+        spot = piece(j, at, x, k)
+        return copy(
+            spot if source is None else source, spot,
+            line_send.at[j, at], line_recv.at[j, at], "ctx", to,
+        )
+
+    def to_across(j, at, side, source=None):
+        spot = piece(j, at, side, k)
+        return copy(
+            spot if source is None else source, spot,
+            cross_send.at[j, at], cross_recv.at[j, at], "batch", across,
+        )
+
+    def to_pair(j, at, side, core, source=None):
+        spot = piece(j, at, side, core)
+        return copy(
+            spot if source is None else source, spot,
+            pair_send.at[j, at, side], pair_recv.at[j, at, side], "batch", partner,
+        )
+
+    swap = copy(
+        slab_ref.at[other], out.at[me, c, x, k], side_send.at[0], side_recv.at[0], "head", other
+    )
+    tok_swap = copy(tok_ref, tok_out.at[me], side_send.at[1], side_recv.at[1], "head", other)
+    cot_swap = copy(cot_ref, cot_out.at[me], side_send.at[2], side_recv.at[2], "head", other)
+    swap.start()
+
+    def own(j, source):
+        to_across(j, c, x, source).start()
+
+        @pl.when(c < n - 1)
+        def _():
+            copy(
+                source, piece(j, c, x, k), own_sem.at[3 + j], line_recv.at[j, c], "ctx", right
+            ).start()
+
+        @pl.when(c > 0)
+        def _():
+            copy(
+                source, piece(j, c, x, k), own_sem.at[5 + j], line_recv.at[j, c], "ctx", left
+            ).start()
+
+        to_pair(j, c, x, k, source).start()
+
+    kept = slab_ref.at[me]
+    own(0, kept)
+    locals_ = (
+        pltpu.make_async_copy(kept, out.at[me, c, x, k], own_sem.at[0]),
+        pltpu.make_async_copy(tok_ref, tok_out.at[me], own_sem.at[1]),
+        pltpu.make_async_copy(cot_ref, cot_out.at[me], own_sem.at[2]),
+    )
+    for one in locals_:
+        one.start()
+    from_side = copy(
+        slab_ref.at[other], out.at[other, c, x, k], side_send.at[0], side_recv.at[0], "head", other
+    )
+    from_side.wait_recv()
+    own(1, piece(1, c, x, k))
+    tok_swap.start()
+    cot_swap.start()
+
+    def cross_done(j, at):
+        to_across(j, at, 1 - x).wait_recv()
+        to_pair(j, at, 1 - x, k).start()
+
+    for distance in range(1, n + 1):
+        for j in range(2):
+            for sign in (-1, 1):
+                at = c + sign * distance
+                back = c + sign * (distance - 1)
+                onward = right if sign < 0 else left
+                more = (c < n - 1) if sign < 0 else (c > 0)
+                if distance < n:
+
+                    @pl.when((at >= 0) & (at < n))
+                    def _():
+                        to_line(j, at, onward).wait_recv()
+
+                        @pl.when(more)
+                        def _():
+                            to_line(j, at, onward).start()
+
+                        to_across(j, at, x).start()
+                        to_pair(j, at, x, k).start()
+
+                if distance > 1:
+
+                    @pl.when((back >= 0) & (back < n))
+                    def _():
+                        cross_done(j, back)
+
+                elif sign < 0:
+                    cross_done(j, c)
+
+    for j in range(2):
+
+        def settle(at, carry):
+            for side in range(2):
+                to_pair(j, at, side, 1 - k).wait_recv()
+                to_pair(j, at, side, k).wait_send()
+            to_across(j, at, x).wait_send()
+
+            @pl.when(((at < c) & (c < n - 1)) | ((at > c) & (c > 0)))
+            def _():
+                to_line(j, at, right).wait_send()
+
+            return carry
+
+        lax.fori_loop(0, n, settle, 0)
+        spot = piece(j, c, x, k)
+
+        @pl.when(c < n - 1)
+        def _():
+            copy(spot, spot, own_sem.at[3 + j], line_recv.at[j, c], "ctx", right).wait_send()
+
+        @pl.when(c > 0)
+        def _():
+            copy(spot, spot, own_sem.at[5 + j], line_recv.at[j, c], "ctx", left).wait_send()
+
+    for one in locals_:
+        one.wait()
+    swap.wait_send()
+    for sent, target, slot in ((tok_swap, tok_out, 1), (cot_swap, cot_out, 2)):
+        sent.wait_send()
+        copy(
+            target.at[other], target.at[other], side_send.at[slot], side_recv.at[slot], "head", other
+        ).wait_recv()
+
+
+def gathers(slabs):
+    return (
+        lax.axis_size("head") == 2
+        and lax.axis_size("batch") == 2 * PAIR
+        and slabs.shape[1] % 16 == 0
+    )
+
+
+def gather_all(slabs, tok, cot):
+    n = lax.axis_size("ctx")
+    rows, cols = slabs.shape[1:]
+    vmem = pl.BlockSpec(memory_space=pltpu.VMEM)
+    anywhere = pl.BlockSpec(memory_space=pl.ANY)
+    dma = pltpu.SemaphoreType.DMA
+    half = jnp.bfloat16
+    weight, tokens, cots = pl.pallas_call(
+        functools.partial(gather_kernel, n),
+        in_specs=[vmem] * 3,
+        out_specs=[anywhere] * 3,
+        out_shape=[
+            of_shape((2, n, 2, 2, rows, cols), half),
+            of_shape((2,) + tok.shape, half),
+            of_shape((2,) + cot.shape, half),
+        ],
+        scratch_shapes=[
+            dma((7,)), dma((3,)), dma((3,)), dma((2, n)), dma((2, n)),
+            dma((2, n)), dma((2, n)), dma((2, n, 2)), dma((2, n, 2)),
+        ],
+        compiler_params=pltpu.CompilerParams(collective_id=1, has_side_effects=True),
+        cost_estimate=pl.CostEstimate(
+            flops=0, bytes_accessed=64 * n * rows * cols, transcendentals=0
+        ),
+    )(slabs, tok, cot)
+    return (
+        weight.reshape(8 * n * rows, cols),
+        tokens.reshape(-1, tok.shape[1]),
+        cots.reshape(-1, cot.shape[1]),
+    )
+
+
+def outer_kernel(*refs):
+    out = refs[-1]
+    first = 0
+    for left_ref, right_ref in zip(refs[:-1:2], refs[1:-1:2]):
+        width = right_ref.shape[1]
+        part = one_pass(left_ref[...], right_ref[...], 0, 0)
+        out[:, first : first + width] = part.astype(out.dtype)
+        first += width
+
+
+def outer_products(*pairs):
+    tokens, features = pairs[0][0].shape
+    block = min(256, features)
+    total = sum(second.shape[1] for _, second in pairs)
+    specs = []
+    for _, second in pairs:
+        specs.append(pl.BlockSpec((tokens, block), lambda i: (0, i)))
+        specs.append(pl.BlockSpec(second.shape, lambda i: (0, 0)))
+    args = [one for pair in pairs for one in pair]
+    return pl.pallas_call(
+        outer_kernel,
+        grid=(features // block,),
+        in_specs=specs,
+        out_specs=pl.BlockSpec((block, total), lambda i: (i, 0)),
+        out_shape=of_shape((features, total), jnp.bfloat16),
+        cost_estimate=pl.CostEstimate(
+            flops=2 * tokens * features * total,
+            bytes_accessed=2 * features * total,
+            transcendentals=0,
+        ),
+    )(*args)
 
 
 def body(
@@ -381,25 +887,29 @@
     slabs_in = head_halves(
         [w_query, w_key, w_value, w_gate, w_rates, jnp.tile(gains, (1, parts))], parts
     )
-    in_weight = whole_rows(swap_halves(slabs_in))
     rates_width = w_rates.shape[1] // parts
     mixed_width = 2 * query_width + value_width
     proj_width = mixed_width + value_width + rates_width
+    later = swap_halves(head_halves([w_out, w_ffgate, w_ffup, w_down], parts))
+    ff_local = w_down.shape[1] // parts
+    if gathers(slabs_in):
+        later, slabs_in = lax.optimization_barrier((later, slabs_in))
+        later_weight = whole_rows(later)
+        in_weight, piece_tok, cot = gather_all(slabs_in, tokens[0], cotangent[0])
+    else:
+        in_weight = whole_rows(swap_halves(slabs_in))
+        later_weight = whole_rows(later)
+        piece_tok = lax.all_gather(tokens[0], "head", axis=0, tiled=True)
+        cot = lax.all_gather(cotangent[0], "head", axis=0, tiled=True)
     gain_cols = in_weight[:, proj_width:].astype(jnp.float32)
     gain_one = gain_cols[:, 0]
     gain_two = gain_cols[:, 1]
-    later = swap_halves(head_halves([w_out, w_ffgate, w_ffup, w_down], parts))
-    ff_local = w_down.shape[1] // parts
-    later_weight = whole_rows(later)
     out_weight = later_weight[:, :value_width]
     ff_weight = later_weight[:, value_width : value_width + 2 * ff_local]
     down_weight = later_weight[:, value_width + 2 * ff_local :]
 
     inputs_tok = tokens[0]
     own_count = inputs_tok.shape[0]
-    piece_tok = lax.all_gather(inputs_tok, "head", axis=0, tiled=True)
-    cot = lax.all_gather(cotangent[0], "head", axis=0, tiled=True)
-    piece_tok, cot = lax.optimization_barrier((piece_tok, cot))
     residual = piece_tok.astype(jnp.float32)
     piece_rows = residual.shape[0]
     normed_one = rms_scale(residual, gain_one).astype(jnp.bfloat16)
@@ -520,15 +1030,9 @@
         lasts.insert(0, chunk_reach[i] + state_pull(chunk_maps[i], lasts[0]))
     last_grads = jnp.stack(lasts, axis=1)
 
-    ff_products = jnp.concatenate(
-        [
-            mat_tn(middle_grad_b, gated).astype(jnp.bfloat16),
-            mat_tn(normed_two, ff_grads).astype(jnp.bfloat16),
-            mat_tn(cot, hidden).astype(jnp.bfloat16),
-        ],
-        axis=1,
-    )
-    last_grads, ff_products = lax.optimization_barrier((last_grads, ff_products))
+    ff_products = outer_products(
+        (middle_grad_b, gated), (normed_two, ff_grads), (cot, hidden)
+    )
     ff_sums = lax.psum_scatter(
         ff_products,
         ("ctx", "batch"),
@@ -560,20 +1064,7 @@
         [own_rows[: piece_rows - margin], own_rows[piece_rows - margin :] + back_rim], axis=0
     ).astype(jnp.bfloat16)
     proj_grad = jnp.concatenate([own_rows, gate_bf, rates_grad_f.astype(jnp.bfloat16)], axis=1)
-    proj_products = mat_tn(normed_one, proj_grad).astype(jnp.bfloat16)
-    proj_products, ff_sums = lax.optimization_barrier((proj_products, ff_sums))
-    ff_parts = split_columns(
-        ff_sums.astype(jnp.float32), (value_width, ff_local, ff_local, ff_local)
-    )
-    proj_sums = lax.psum_scatter(
-        proj_products,
-        ("ctx", "batch"),
-        scatter_dimension=0,
-        tiled=True,
-    ).astype(jnp.float32)
-    proj_parts = split_columns(
-        proj_sums, (query_width, query_width, value_width, value_width, rates_width)
-    )
+    proj_products = outer_products((normed_one, proj_grad))
     own_grad = own_rows_sum(mat_nt(proj_grad, in_weight[:, :proj_width]))
     unused_rows, norm_one_vjp = jax.vjp(rms_scale, inputs_tok.astype(jnp.float32), gain_one)
     input_part, gain_one_grad = norm_one_vjp(own_grad)
@@ -586,7 +1077,18 @@
         decay_log_grad,
         decay_bias_grad,
     )
-    summed = lax.psum(jnp.concatenate(smalls), ("ctx", "batch"))
+    proj_widths = (query_width, query_width, value_width, value_width, rates_width)
+    if staged(proj_products.shape[0]):
+        proj_parts, summed = scatter_sum(proj_products, jnp.concatenate(smalls), proj_widths)
+    else:
+        proj_sums = lax.psum_scatter(
+            proj_products, ("ctx", "batch"), scatter_dimension=0, tiled=True
+        ).astype(jnp.float32)
+        proj_parts = split_columns(proj_sums, proj_widths)
+        summed = lax.psum(jnp.concatenate(smalls), ("ctx", "batch"))
+    ff_parts = split_columns(
+        ff_sums.astype(jnp.float32), (value_width, ff_local, ff_local, ff_local)
+    )
     cuts = []
     first = 0
     for small in smalls:

time: 523 us -> 430 us (0.82)
  Pallas kernels: 77.3 us -> 229 us
  waiting for transfers between devices: 178 us -> 70.1 us
  blocking collectives: 98.6 us -> 0 us
  matrix products: 46 us -> 32.8 us
  local copies, waits for them, and re-layouts: 40.1 us -> 28.1 us
  starting transfers between devices: 32.5 us -> 25.3 us
    pallas_call x0 -> x4, Pallas kernels: none -> 180 us  [the longest x1 91.3 us: scatter_sum(): pl.pallas_call(functools.partial(scatter_kernel, n, steps, widths), in_sp...]
    reduce_scatter x1, waiting for transfers between devices: 76.8 us -> 0.01 us  [body(): lax.psum_scatter(ff_products, ('ctx', 'batch'), scatter_dimension=0, tile...]
    psum x1 -> x0, blocking collectives: 60.4 us -> none  [body(): summed = lax.psum(jnp.concatenate(smalls), ('ctx', 'batch'))]
    all_gather x2 -> x1, waiting for transfers between devices: 36 us -> 0.01 us  [whole_rows(): full = lax.all_gather(slabs, ('ctx', 'batch'), axis=1, tiled=True)]
    pallas_call x4, Pallas kernels: 77.3 us -> 48.5 us  [per_head(): pl.pallas_call(kernel, grid=grid, in_specs=ins, out_specs=[spec for spec,...]
    all_to_all x2 -> x0, blocking collectives: 23.8 us -> none  [swap_halves(): lax.all_to_all(slabs, 'head', split_axis=0, concat_axis=0, tiled=True)]
    dot_general x4 -> x0, matrix products: 15.1 us -> none  [mat_tn(): lax.dot_general(first_mat, second_mat, (((0,), (0,)), ((), ())), preferre...]
    all_gather x2 -> x0, blocking collectives: 14.3 us -> none  [the longest x1 7.3 us: body(): cot = lax.all_gather(cotangent[0], 'head', axis=0, tiled=True)]
  transfers between devices with their start and end apart: 17 -> 16, of which waited for: 13 -> 12; matrix products, arithmetic and copies ran while one was open for 14% -> 14% of each run, Pallas kernels for 14% -> 51%
where the time goes in v1:
time: 430 us; the launch traced here: 428 us
  Pallas kernels  229 us (53%)
  waiting for transfers between devices  70.1 us (16%)
  matrix products  32.8 us (8%)
  other arithmetic  28.3 us (7%)
  local copies, waits for them, and re-layouts  28.1 us (7%)
  starting transfers between devices  25.3 us (6%)
  between operations  15 us (3%)
    pallas_call x1, Pallas kernels, scatter_sum(): pl.pallas_call(functools.partial(scatter_kernel, n, steps, widths), in_sp...  91.3 us
    pallas_call x1, Pallas kernels, gather_all(): pl.pallas_call(functools.partial(gather_kernel, n), in_specs=[vmem] * 3,...  74.2 us
    pallas_call x4, Pallas kernels, per_head(): pl.pallas_call(kernel, grid=grid, in_specs=ins, out_specs=[spec for spec,...  48.5 us
    ppermute x8, waiting for transfers between devices, passed_along(): return lax.ppermute(block, axis, route)  41.5 us
    ppermute x3, waiting for transfers between devices, other_parts(): lax.ppermute(block, 'head', [(i, (i + shift) % parts) for i in range(part...  22 us
    ppermute x8, starting transfers between devices, passed_along(): return lax.ppermute(block, axis, route)  19.2 us
    dot_general x4, matrix products, mat_nn(): return jnp.dot(first_mat, second_mat, preferred_element_type=jnp.float32)  15.2 us
    pallas_call x2, Pallas kernels, outer_products(): pl.pallas_call(outer_kernel, grid=(features // block,), in_specs=specs, o...  14.6 us
  transfers between devices with their start and end apart: 16, of which 12 were waited for; matrix products, arithmetic and copies ran while one was open for 14% of the time, Pallas kernels for 51%

profile of v1, /device:TPU:0, one launch (start us, length us, event | category | flops | bytes accessed | tf_op | source)
XLA Modules:
  0.0 428.1 jit_solution(1570277025378406792)
XLA Ops:
  11.5 3.1 collective-permute-start
  16.1 6.3 %collective-permute-done = bf16[32,5248]{1,0:T(8,128)(2,1)S(1)} collective-permute-done((bf16[32,5248]{1,0:T(8,128)(2,1)S(1)}, bf16[32,5248]{1,0:T(8,128)(2,1)S(1)}, u32[]{:S(2)}, u32[]{:S(2)}) %collective-permute-start) | collective-permute-done | bytes 335904 | tf_op jit(solution)/shard_map/ppermute | solution.py:331
  23.6 74.2 %shard_map.330 = (bf16[2,4,2,2,32,3082]{5,4,3,2,1,0:T(8,128)(2,1)}, bf16[2,128,1024]{2,1,0:T(8,128)(2,1)}, bf16[2,128,1024]{2,1,0:T(8,128)(2,1)}) custom-call(bf16[2,32,3082]{2,1,0:T(8,128)(2,1)} %pad_maximum_fusion.2.slab_ref, bf16[128,1024]{1,0:T(8,128)(2,1)} %bitcast.131, bf16[128,1024]{1,0:T(8,128)(2,1)} %bitcast.137), custom_call_target="tpu_custom_call" | custom-call | bytes 25247744 | tf_op jit(solution)/shard_map/pallas_call | solution.py:799
  101.5 5.0 %fusion.4.gate_ref = bf16[256,3080]{1,0:T(8,128)(2,1)S(1)} fusion(bf16[256,1024]{1,0:T(8,128)(2,1)S(1)} %fusion.39.refs_0_, bf16[1024,3082]{1,0:T(8,128)(2,1)} %bitcast.169), kind=kOutput, calls=%fused_computation.4 | convolution fusion | flops 1615595520 | bytes 8413184 | tf_op jit(solution)/shard_map/dot_general | solution.py:277
  110.9 2.3 multiply_add_fusion.q_ref.k_ref.v_ref
  113.2 23.0 %shard_map.331 = (f32[4,1,256,256]{3,2,1,0:T(8,128)}, f32[256,1024]{1,0:T(8,128)}, f32[256,512]{1,0:T(8,128)}, f32[4,1,128,128]{3,2,1,0:T(8,128)}, f32[4,1,128,256]{3,2,1,0:T(8,128)}) custom-call(f32[256,2048]{1,0:T(8,128)} %multiply_add_fusion.q_ref.k_ref.v_ref, f32[256,2048]{1,0:T(8,128)} %multiply_add_fusion.q_ref.k_ref.v_ref, ...), custom_call_target="tpu_custom_call" | custom-call | flops 6710886400 | bytes 6299648 | tf_op jit(solution)/shard_map/pallas_call | solution.py:232
  137.4 3.4 collective-permute-start.2
  140.8 5.6 %collective-permute-done.2 = bf16[4,128,256]{2,1,0:T(8,128)(2,1)S(1)} collective-permute-done((bf16[4,128,256]{2,1,0:T(8,128)(2,1)S(1)}, bf16[4,128,256]{2,1,0:T(8,128)(2,1)S(1)}, u32[]{:S(2)}, u32[]{:S(2)}) %collective-permute-start.2) | collective-permute-done | bytes 262176 | tf_op jit(solution)/shard_map/ppermute | solution.py:20
  147.9 4.4 %collective-permute-start.3 = (bf16[4,128,256]{2,1,0:T(8,128)(2,1)S(1)}, bf16[4,128,256]{2,1,0:T(8,128)(2,1)S(1)}, u32[]{:S(2)}, u32[]{:S(2)}) collective-permute-start(bf16[4,128,256]{2,1,0:T(8,128)(2,1)S(1)} %fusion.32), channel_id=1, source_target_pairs={{0,4},{4,8},{8,12},{1,5},{5,9},{9,13},{2,6},{6,10},{10,14},{3,7},{... | collective-permute-start | bytes 786440 | tf_op jit(solution)/shard_map/ppermute | solution.py:20
  152.3 4.8 %collective-permute-done.3 = bf16[4,128,256]{2,1,0:T(8,128)(2,1)S(1)} collective-permute-done((bf16[4,128,256]{2,1,0:T(8,128)(2,1)S(1)}, bf16[4,128,256]{2,1,0:T(8,128)(2,1)S(1)}, u32[]{:S(2)}, u32[]{:S(2)}) %collective-permute-start.3) | collective-permute-done | bytes 262176 | tf_op jit(solution)/shard_map/ppermute | solution.py:20
  157.4 4.6 %collective-permute-start.4 = (bf16[4,128,256]{2,1,0:T(8,128)(2,1)S(1)}, bf16[4,128,256]{2,1,0:T(8,128)(2,1)S(1)}, u32[]{:S(2)}, u32[]{:S(2)}) collective-permute-start(bf16[4,128,256]{2,1,0:T(8,128)(2,1)S(1)} %fusion.33), channel_id=1, source_target_pairs={{0,4},{4,8},{8,12},{1,5},{5,9},{9,13},{2,6},{6,10},{10,14},{3,7},{... | collective-permute-start | bytes 786440 | tf_op jit(solution)/shard_map/ppermute | solution.py:20
  162.6 3.1 collective-permute-done.4
  166.6 4.3 %shard_map.332.refs_1_ = bf16[256,1024]{1,0:T(8,128)(2,1)} custom-call(f32[256,1024]{1,0:T(8,128)} %get-tuple-element.47.o_ref, f32[256,512]{1,0:T(8,128)} %get-tuple-element.48.e_ref, f32[4,1,128,256]{3,2,1,0:T(8,128)} %bitcast_convert_fusion.3.i_ref, bf16[256,3080]{1,0:T(8,128)(2,1)} %copy-done.5, f32[1,1024]{1,0:T(1,128)} %bitcast.161), custom_call_target="tpu_custom_call" | custom-call | flops 402653184 | bytes 3678208 | tf_op jit(solution)/shard_map/pallas_call | solution.py:232
  170.9 2.5 fusion.23
  173.5 11.1 %collective-permute-done.5 = bf16[256,1024]{1,0:T(8,128)(2,1)S(1)} collective-permute-done((bf16[256,1024]{1,0:T(8,128)(2,1)S(1)}, bf16[256,1024]{1,0:T(8,128)(2,1)S(1)}, u32[]{:S(2)}, u32[]{:S(2)}) %collective-permute-start.5) | collective-permute-done | bytes 524320 | tf_op jit(solution)/shard_map/ppermute | solution.py:345
  185.2 4.6 %fusion.9 = f32[256,2816]{1,0:T(8,128)S(1)} fusion(bf16[256,1024]{1,0:T(8,128)(2,1)S(1)} %multiply_convert_fusion.2.refs_2_, bf16[1024,5248]{1,0:T(8,128)(2,1)} %bitcast.174), kind=kOutput, calls=%fused_computation.7 | convolution fusion | flops 1476395008 | bytes 9175040 | tf_op jit(solution)/shard_map/dot_general | solution.py:277
  191.0 2.3 fusion.21
  196.6 8.8 %collective-permute-done.7 = bf16[256,1024]{1,0:T(8,128)(2,1)S(1)} collective-permute-done((bf16[256,1024]{1,0:T(8,128)(2,1)S(1)}, bf16[256,1024]{1,0:T(8,128)(2,1)S(1)}, u32[]{:S(2)}, u32[]{:S(2)}) %collective-permute-start.7) | collective-permute-done | bytes 524320 | tf_op jit(solution)/shard_map/ppermute | solution.py:345
  207.3 8.4 %shard_map.337 = bf16[1024,5248]{1,0:T(8,128)(2,1)} custom-call(bf16[256,1024]{1,0:T(8,128)(2,1)} %get-tuple-element.155.refs_0_, bf16[256,1024]{1,0:T(8,128)(2,1)} %shard_map.332.refs_1_, bf16[256,1024]{1,0:T(8,128)(2,1)} %copy-done.15, bf16[256,2816]{1,0:T(8,128)(2,1)} %pad_maximum_fusion.1.refs_3_, bf16[256,1024]{1,0:T(8,128)(2,1)} %bitcast.132, ...), custom_call_target="tpu_custom_call" | custom-call | flops 2751463424 | bytes 10747904 | tf_op jit(solution)/shard_map/pallas_call | solution.py:843
  215.7 3.3 fusion.26.grad_ref
  219.0 5.5 %shard_map.333 = (f32[256,1024]{1,0:T(8,128)}, bf16[256,1024]{1,0:T(8,128)(2,1)}, f32[1,1,1024]{2,1,0:T(1,128)}, f32[4,1,128,256]{3,2,1,0:T(8,128)}) custom-call(f32[256,1024]{1,0:T(8,128)} %get-tuple-element.47.o_ref, f32[256,512]{1,0:T(8,128)} %get-tuple-element.48.e_ref, f32[4,1,128,256]{3,2,1,0:T(8,128)} %bitcast_convert_fusion.3.i_ref, ...), custom_call_target="tpu_custom_call" | custom-call | flops 805306368 | bytes 4202496 | tf_op jit(solution)/shard_map/pallas_call | solution.py:232
  228.8 6.9 %collective-permute-done.8 = bf16[4,128,256]{2,1,0:T(8,128)(2,1)} collective-permute-done((bf16[4,128,256]{2,1,0:T(8,128)(2,1)}, bf16[4,128,256]{2,1,0:T(8,128)(2,1)}, u32[]{:S(2)}, u32[]{:S(2)}) %collective-permute-start.8) | collective-permute-done | bytes 262176 | tf_op jit(solution)/shard_map/ppermute | solution.py:20
  238.8 3.2 fusion.13
  243.3 3.4 collective-permute-done.9
  249.6 1.9 fusion.51
  251.5 16.6 %collective-permute-done.10 = bf16[4,128,256]{2,1,0:T(8,128)(2,1)S(1)} collective-permute-done((bf16[4,128,256]{2,1,0:T(8,128)(2,1)}, bf16[4,128,256]{2,1,0:T(8,128)(2,1)S(1)}, u32[]{:S(2)}, u32[]{:S(2)}) %collective-permute-start.10) | collective-permute-done | bytes 262176 | tf_op jit(solution)/shard_map/ppermute | solution.py:20
  268.9 15.6 %shard_map.334 = (f32[256,512]{1,0:T(8,128)}, f32[256,512]{1,0:T(8,128)}, f32[256,1024]{1,0:T(8,128)}, f32[4,1,256,1]{3,2,1,0:T(8,128)}, f32[4,1,256,1]{3,2,1,0:T(8,128)}) custom-call(f32[256,2048]{1,0:T(8,128)} %multiply_add_fusion.q_ref.k_ref.v_ref, f32[256,2048]{1,0:T(8,128)} %multiply_add_fusion.q_ref.k_ref.v_ref, ...), custom_call_target="tpu_custom_call" | custom-call | flops 6710886400 | bytes 9445376 | tf_op jit(solution)/shard_map/pallas_call | solution.py:232
  298.1 5.6 %fusion = f32[256,1024]{1,0:T(8,128)S(1)} fusion(bf16[256,3080]{1,0:T(8,128)(2,1)S(1)} %pad_maximum_fusion.refs_1_, bf16[1024,3082]{1,0:T(8,128)(2,1)} %bitcast.170), kind=kOutput, calls=%fused_computation | convolution fusion | flops 1614807040 | bytes 8937472 | tf_op jit(solution)/shard_map/dot_general | solution.py:265
  305.4 6.2 %shard_map.335 = bf16[1024,3080]{1,0:T(8,128)(2,1)} custom-call(bf16[256,1024]{1,0:T(8,128)(2,1)} %copy-done.13, bf16[256,3080]{1,0:T(8,128)(2,1)} %copy-done.6), custom_call_target="tpu_custom_call" | custom-call | flops 1614807040 | bytes 6307840 | tf_op jit(solution)/shard_map/pallas_call | solution.py:843
  313.5 2.1 collective-permute-done.13
  316.3 91.3 %shard_map.336 = (f32[4,16,512]{2,1,0:T(8,128)}, f32[4,16,512]{2,1,0:T(8,128)}, f32[4,16,1024]{2,1,0:T(8,128)}, f32[4,16,1024]{2,1,0:T(8,128)}, f32[4,16,8]{2,1,0:T(8,128)}, /*index=5*/f32[96,128]{1,0:T(8,128)}) custom-call(bf16[4,2,2,4,16,3080]{5,4,3,2,1,0:T(8,128)(2,1)} %bitcast.130, f32[96,128]{1,0:T(8,128)} %pad_bitcast_fusion.sm_ref), custom_call_target="tpu_custom_call" | custom-call | bytes 25231360 | tf_op jit(solution)/shard_map/pallas_call | solution.py:604
  416.5 2.1 fusion.74
  (197 shorter events, 67.6 us)
Async XLA Ops:
  7.2 7.5 %copy-start.35 = (bf16[32]{0:T(256)(128)(2,1)S(1)}, bf16[32]{0:T(256)(128)(2,1)}, u32[]{:S(2)}) copy-start(bf16[32]{0:T(256)(128)(2,1)} %param.34) | copy-start | bytes 196
  7.2 7.8 %copy-start.25 = (bf16[32,1024]{1,0:T(8,128)(2,1)S(1)}, bf16[32,1024]{1,0:T(8,128)(2,1)}, u32[]{:S(2)}) copy-start(bf16[32,1024]{1,0:T(8,128)(2,1)} %param.23) | copy-start | bytes 196612
  7.2 7.8 %copy-start.26 = (bf16[32,1024]{1,0:T(8,128)(2,1)S(1)}, bf16[32,1024]{1,0:T(8,128)(2,1)}, u32[]{:S(2)}) copy-start(bf16[32,1024]{1,0:T(8,128)(2,1)} %param.22) | copy-start | bytes 196612
  7.2 163.7 %all-gather.2.cloned.1.call-start = ((), (), s32[]{:S(2)}) async-start(), calls=%async_computation.1 | async-start | bytes 11419648 | tf_op jit(solution)/shard_map/all_gather | solution.py:337
  11.5 10.9 %collective-permute-start = (bf16[32,5248]{1,0:T(8,128)(2,1)S(1)}, bf16[32,5248]{1,0:T(8,128)(2,1)S(1)}, u32[]{:S(2)}, u32[]{:S(2)}) collective-permute-start(bf16[32,5248]{1,0:T(8,128)(2,1)S(1)} %get-tuple-element.170), channel_id=1, source_target_pairs={{0,16},{16,0},{1,17},{17,1},{2,18},{18,2},{3,19},{19,3},{4,20},{20... | collective-permute-start | bytes 1007624 | tf_op jit(solution)/shard_map/ppermute | solution.py:331
  15.0 8.4 %copy-start.37 = (f32[4]{0:T(128)S(1)}, f32[4]{0:T(128)}, u32[]{:S(2)}) copy-start(f32[4]{0:T(128)} %param.30) | copy-start | bytes 52
  15.1 8.4 %copy-start.27 = (bf16[4,1024]{1,0:T(4,128)(2,1)S(1)}, bf16[4,1024]{1,0:T(4,128)(2,1)}, u32[]{:S(2)}) copy-start(bf16[4,1024]{1,0:T(4,128)(2,1)} %param.29) | copy-start | bytes 24580
  15.1 8.4 %copy-start.29 = (bf16[4,512]{1,0:T(4,128)(2,1)S(1)}, bf16[4,512]{1,0:T(4,128)(2,1)}, u32[]{:S(2)}) copy-start(bf16[4,512]{1,0:T(4,128)(2,1)} %param.28) | copy-start | bytes 12292
  15.1 8.4 %copy-start.30 = (bf16[4,512]{1,0:T(4,128)(2,1)S(1)}, bf16[4,512]{1,0:T(4,128)(2,1)}, u32[]{:S(2)}) copy-start(bf16[4,512]{1,0:T(4,128)(2,1)} %param.27) | copy-start | bytes 12292
  23.4 391.4 %reduce-scatter.2.cloned.1.call-start = ((), (), s32[]{:S(2)}) async-start(), calls=%async_computation.2 | async-start | bytes 11419648 | tf_op jit(solution)/shard_map/reduce_scatter | solution.py:1036
  106.6 4.0 collective-permute-start.1
  136.2 20.9 %copy-start.9 = (f32[4,1,128,256]{3,2,1,0:T(8,128)S(1)}, f32[4,1,128,256]{3,2,1,0:T(8,128)}, u32[]{:S(2)}) copy-start(f32[4,1,128,256]{3,2,1,0:T(8,128)} %get-tuple-element.49) | copy-start | bytes 1572868
  136.2 20.9 %copy-start.10 = (f32[4,1,128,128]{3,2,1,0:T(8,128)S(1)}, f32[4,1,128,128]{3,2,1,0:T(8,128)}, u32[]{:S(2)}) copy-start(f32[4,1,128,128]{3,2,1,0:T(8,128)} %get-tuple-element.50) | copy-start | bytes 786436
  136.2 25.8 %copy-start.33 = (bf16[1024]{0:T(1024)(128)(2,1)S(1)}, bf16[1024]{0:T(1024)(128)(2,1)}, u32[]{:S(2)}) copy-start(bf16[1024]{0:T(1024)(128)(2,1)} %param.32) | copy-start | bytes 6148
  137.4 9.0 %collective-permute-start.2 = (bf16[4,128,256]{2,1,0:T(8,128)(2,1)S(1)}, bf16[4,128,256]{2,1,0:T(8,128)(2,1)S(1)}, u32[]{:S(2)}, u32[]{:S(2)}) collective-permute-start(bf16[4,128,256]{2,1,0:T(8,128)(2,1)S(1)} %bitcast_convert_fusion.1), channel_id=1, source_target_pairs={{0,4},{4,8},{8,12},{1,5},{5,9},{9,13},{2,6},{6,10},{10,14},{3,7},{... | collective-permute-start | bytes 786440 | tf_op jit(solution)/shard_map/ppermute | solution.py:20
  147.9 9.2 %collective-permute-start.3 = (bf16[4,128,256]{2,1,0:T(8,128)(2,1)S(1)}, bf16[4,128,256]{2,1,0:T(8,128)(2,1)S(1)}, u32[]{:S(2)}, u32[]{:S(2)}) collective-permute-start(bf16[4,128,256]{2,1,0:T(8,128)(2,1)S(1)} %fusion.32), channel_id=1, source_target_pairs={{0,4},{4,8},{8,12},{1,5},{5,9},{9,13},{2,6},{6,10},{10,14},{3,7},{... | collective-permute-start | bytes 786440 | tf_op jit(solution)/shard_map/ppermute | solution.py:20
  157.4 8.3 %collective-permute-start.4 = (bf16[4,128,256]{2,1,0:T(8,128)(2,1)S(1)}, bf16[4,128,256]{2,1,0:T(8,128)(2,1)S(1)}, u32[]{:S(2)}, u32[]{:S(2)}) collective-permute-start(bf16[4,128,256]{2,1,0:T(8,128)(2,1)S(1)} %fusion.33), channel_id=1, source_target_pairs={{0,4},{4,8},{8,12},{1,5},{5,9},{9,13},{2,6},{6,10},{10,14},{3,7},{... | collective-permute-start | bytes 786440 | tf_op jit(solution)/shard_map/ppermute | solution.py:20
  170.9 13.8 %copy-start.7 = (bf16[2,128,1024]{2,1,0:T(8,128)(2,1)S(1)}, bf16[2,128,1024]{2,1,0:T(8,128)(2,1)}, u32[]{:S(2)}) copy-start(bf16[2,128,1024]{2,1,0:T(8,128)(2,1)} %get-tuple-element.45) | copy-start | bytes 1572868
  173.5 11.2 %collective-permute-start.5 = (bf16[256,1024]{1,0:T(8,128)(2,1)S(1)}, bf16[256,1024]{1,0:T(8,128)(2,1)S(1)}, u32[]{:S(2)}, u32[]{:S(2)}) collective-permute-start(bf16[256,1024]{1,0:T(8,128)(2,1)S(1)} %fusion.23), channel_id=1, source_target_pairs={{0,16},{16,0},{1,17},{17,1},{2,18},{18,2},{3,19},{19,3},{4,20},{20... | collective-permute-start | bytes 1572872 | tf_op jit(solution)/shard_map/ppermute | solution.py:345
  195.0 10.3 %collective-permute-start.7 = (bf16[256,1024]{1,0:T(8,128)(2,1)S(1)}, bf16[256,1024]{1,0:T(8,128)(2,1)S(1)}, u32[]{:S(2)}, u32[]{:S(2)}) collective-permute-start(bf16[256,1024]{1,0:T(8,128)(2,1)S(1)} %fusion.29), channel_id=1, source_target_pairs={{0,16},{16,0},{1,17},{17,1},{2,18},{18,2},{3,19},{19,3},{4,20},{20... | collective-permute-start | bytes 1572872 | tf_op jit(solution)/shard_map/ppermute | solution.py:345
  226.4 9.3 %collective-permute-start.8 = (bf16[4,128,256]{2,1,0:T(8,128)(2,1)}, bf16[4,128,256]{2,1,0:T(8,128)(2,1)}, u32[]{:S(2)}, u32[]{:S(2)}) collective-permute-start(bf16[4,128,256]{2,1,0:T(8,128)(2,1)} %bitcast_convert_fusion), channel_id=1, source_target_pairs={{4,0},{8,4},{12,8},{5,1},{9,5},{13,9},{6,2},{10,6},{14,10},{7,3},{... | collective-permute-start | bytes 786440 | tf_op jit(solution)/shard_map/ppermute | solution.py:20
  237.4 9.3 %copy-start.8 = (f32[4,1,128,256]{3,2,1,0:T(8,128)S(1)}, f32[4,1,128,256]{3,2,1,0:T(8,128)}, u32[]{:S(2)}) copy-start(f32[4,1,128,256]{3,2,1,0:T(8,128)} %get-tuple-element.55) | copy-start | bytes 1572868
  237.4 9.3 %collective-permute-start.9 = (bf16[4,128,256]{2,1,0:T(8,128)(2,1)S(1)}, bf16[4,128,256]{2,1,0:T(8,128)(2,1)S(1)}, u32[]{:S(2)}, u32[]{:S(2)}) collective-permute-start(bf16[4,128,256]{2,1,0:T(8,128)(2,1)S(1)} %fusion.34), channel_id=1, source_target_pairs={{4,0},{8,4},{12,8},{5,1},{9,5},{13,9},{6,2},{10,6},{14,10},{7,3},{... | collective-permute-start | bytes 786440 | tf_op jit(solution)/shard_map/ppermute | solution.py:20
  242.9 6.7 %collective-permute-start.6 = (bf16[128,1024]{1,0:T(8,128)(2,1)}, bf16[128,1024]{1,0:T(8,128)(2,1)}, u32[]{:S(2)}, u32[]{:S(2)}) collective-permute-start(bf16[128,1024]{1,0:T(8,128)(2,1)} %dynamic-slice_convert_fusion.1), channel_id=1, source_target_pairs={{0,16},{16,0},{1,17},{17,1},{2,18},{18,2},{3,19},{19,3},{4,20},{20... | collective-permute-start | bytes 786440 | tf_op jit(solution)/shard_map/ppermute | solution.py:367
  247.8 20.3 %collective-permute-start.10 = (bf16[4,128,256]{2,1,0:T(8,128)(2,1)}, bf16[4,128,256]{2,1,0:T(8,128)(2,1)S(1)}, u32[]{:S(2)}, u32[]{:S(2)}) collective-permute-start(bf16[4,128,256]{2,1,0:T(8,128)(2,1)} %fusion.35), channel_id=1, source_target_pairs={{4,0},{8,4},{12,8},{5,1},{9,5},{13,9},{6,2},{10,6},{14,10},{7,3},{... | collective-permute-start | bytes 786440 | tf_op jit(solution)/shard_map/ppermute | solution.py:20
  291.1 5.9 %collective-permute-start.11 = (f32[3,2048]{1,0:T(4,128)S(1)}, f32[3,2048]{1,0:T(4,128)S(1)}, u32[]{:S(2)}, u32[]{:S(2)}) collective-permute-start(f32[3,2048]{1,0:T(4,128)S(1)} %pad_add_fusion.1), channel_id=1, source_target_pairs={{4,0},{8,4},{12,8},{5,1},{9,5},{13,9},{6,2},{10,6},{14,10},{7,3},{... | collective-permute-start | bytes 73736 | tf_op jit(solution)/shard_map/ppermute | solution.py:20
  303.8 7.9 %collective-permute-start.12 = (bf16[128,1024]{1,0:T(8,128)(2,1)S(1)}, bf16[128,1024]{1,0:T(8,128)(2,1)S(1)}, u32[]{:S(2)}, u32[]{:S(2)}) collective-permute-start(bf16[128,1024]{1,0:T(8,128)(2,1)S(1)} %dynamic-slice_convert_fusion), channel_id=1, source_target_pairs={{0,16},{16,0},{1,17},{17,1},{2,18},{18,2},{3,19},{19,3},{4,20},{20... | collective-permute-start | bytes 786440 | tf_op jit(solution)/shard_map/ppermute | solution.py:367
  311.9 3.7 collective-permute-start.13
  407.6 11.0 %copy-start.22 = (f32[4,16,512]{2,1,0:T(8,128)S(1)}, f32[4,16,512]{2,1,0:T(8,128)}, u32[]{:S(2)}) copy-start(f32[4,16,512]{2,1,0:T(8,128)} %get-tuple-element.64) | copy-start | bytes 393220
  407.6 11.7 %copy-start.21 = (f32[4,16,512]{2,1,0:T(8,128)S(1)}, f32[4,16,512]{2,1,0:T(8,128)}, u32[]{:S(2)}) copy-start(f32[4,16,512]{2,1,0:T(8,128)} %get-tuple-element.65) | copy-start | bytes 393220
  407.6 12.3 %copy-start.20 = (f32[4,16,1024]{2,1,0:T(8,128)S(1)}, f32[4,16,1024]{2,1,0:T(8,128)}, u32[]{:S(2)}) copy-start(f32[4,16,1024]{2,1,0:T(8,128)} %get-tuple-element.66) | copy-start | bytes 786436
  407.6 13.0 %copy-start.19 = (f32[4,16,1024]{2,1,0:T(8,128)S(1)}, f32[4,16,1024]{2,1,0:T(8,128)}, u32[]{:S(2)}) copy-start(f32[4,16,1024]{2,1,0:T(8,128)} %get-tuple-element.67) | copy-start | bytes 786436
  (22 other events, 107.3 us)
Sparse Core Ops, SparseCore 0:
  23.5 104.9 all-gather.1
  215.9 123.4 reduce-scatter.1

commit v2 on v1

--- a/solution.py
+++ b/solution.py
@@ -508,26 +508,24 @@
             for at in range(n - 1):
                 to_left(q, at).start()
 
-    def relay(q):
-        for near in range(n - 2):
-            far = n - 1 - near
-
-            @pl.when((c > 0) & (c < far))
-            def _():
-                to_right(q, far).wait_recv()
-                total = held[q, far].astype(jnp.float32) + from_left[q, far].astype(jnp.float32)
-                held[q, far] = total.astype(jnp.bfloat16)
-                to_right(q, far).start()
-
-            @pl.when((c < n - 1) & (c > near))
-            def _():
-                to_left(q, near).wait_recv()
-                total = held[q, near].astype(jnp.float32) + from_right[q, near].astype(
-                    jnp.float32
-                )
-                held[q, near] = total.astype(jnp.bfloat16)
-                to_left(q, near).start()
-
+    def relay(hop, q):
+        @pl.when(c == hop)
+        def _():
+            for at in range(n - 1, hop, -1):
+                to_right(q, at).wait_recv()
+                total = held[q, at].astype(jnp.float32) + from_left[q, at].astype(jnp.float32)
+                held[q, at] = total.astype(jnp.bfloat16)
+                to_right(q, at).start()
+
+        @pl.when(c == n - 1 - hop)
+        def _():
+            for at in range(n - 1 - hop):
+                to_left(q, at).wait_recv()
+                total = held[q, at].astype(jnp.float32) + from_right[q, at].astype(jnp.float32)
+                held[q, at] = total.astype(jnp.bfloat16)
+                to_left(q, at).start()
+
+    def finish(q):
         acc[...] = paired[q, x, c].astype(jnp.float32) + from_across[q, c].astype(jnp.float32)
 
         @pl.when(c > 0)
@@ -545,19 +543,32 @@
             out[q] = acc[:, first : first + width]
             first += width
 
-    cross_up(0)
     second_small.wait()
     sm_sent[1] = sm_sent[0] + sm_in[1]
     for shift in range(1, n):
         small_all(shift).start()
 
-    def middle(q, carry):
-        cross_up(q + 1)
-        relay(q)
+    def beat(tick, carry):
+        @pl.when(tick < steps)
+        def _():
+            cross_up(tick)
+
+        for hop in range(1, n - 1):
+            q = tick - hop
+
+            @pl.when((q >= 0) & (q < steps))
+            def _():
+                relay(hop, q)
+
+        last = tick - (n - 1)
+
+        @pl.when(last >= 0)
+        def _():
+            finish(last)
+
         return carry
 
-    lax.fori_loop(0, steps - 1, middle, 0)
-    relay(steps - 1)
+    lax.fori_loop(0, steps + n - 1, beat, 0)
     sm_all[c] = sm_sent[1]
     for shift in range(1, n):
         small_from(shift).wait_recv()
@@ -854,6 +865,81 @@
     )(*args)
 
 
+def chain_kernel(n, forward, map_ref, offset_ref, state_ref, sent, landed, send_sem, recv_sem):
+    c = lax.axis_index("ctx")
+    heads = map_ref.shape[0]
+    place = c if forward else n - 1 - c
+    ahead = jnp.minimum(c + 1, n - 1) if forward else jnp.maximum(c - 1, 0)
+    behind = jnp.maximum(c - 1, 0) if forward else jnp.minimum(c + 1, n - 1)
+    barrier = pltpu.get_barrier_semaphore()
+
+    @pl.when(place > 0)
+    def _():
+        pl.semaphore_signal(barrier, inc=1, device_id={"ctx": behind}, device_id_type=MESH_ID)
+
+    @pl.when(place < n - 1)
+    def _():
+        pl.semaphore_wait(barrier, 1)
+
+    def pass_on(head):
+        return pltpu.make_async_remote_copy(
+            sent.at[head], landed.at[head], send_sem.at[head], recv_sem.at[head],
+            device_id={"ctx": ahead}, device_id_type=MESH_ID,
+        )
+
+    @pl.when(place == 0)
+    def _():
+        sent[...] = offset_ref[...].astype(jnp.bfloat16)
+        for head in range(heads):
+            pass_on(head).start()
+        state_ref[...] = jnp.zeros_like(state_ref)
+
+    @pl.when(place > 0)
+    def _():
+        for head in range(heads):
+            pass_on(head).wait_recv()
+            start = landed[head].astype(jnp.float32)
+
+            @pl.when(place < n - 1)
+            def _():
+                moved = offset_ref[head] + product(
+                    map_ref[head], start, 1 if forward else 0, 0
+                )
+                sent[head] = moved.astype(jnp.bfloat16)
+                pass_on(head).start()
+
+            state_ref[head] = start
+
+    @pl.when(place < n - 1)
+    def _():
+        for head in range(heads):
+            pass_on(head).wait_send()
+
+
+def chain(piece_map, piece_offset, forward):
+    n = lax.axis_size("ctx")
+    heads = piece_map.shape[0]
+    vmem = pl.BlockSpec(memory_space=pltpu.VMEM)
+    dma = pltpu.SemaphoreType.DMA
+    return pl.pallas_call(
+        functools.partial(chain_kernel, n, forward),
+        in_specs=[vmem, vmem],
+        out_specs=vmem,
+        out_shape=of_shape(piece_offset.shape),
+        scratch_shapes=[
+            pltpu.VMEM(piece_offset.shape, jnp.bfloat16),
+            pltpu.VMEM(piece_offset.shape, jnp.bfloat16),
+            dma((heads,)), dma((heads,)),
+        ],
+        compiler_params=pltpu.CompilerParams(
+            collective_id=2 if forward else 3, has_side_effects=True
+        ),
+        cost_estimate=pl.CostEstimate(
+            flops=0, bytes_accessed=8 * n * piece_offset.size, transcendentals=0
+        ),
+    )(piece_map, piece_offset)
+
+
 def body(
     tokens,
     cotangent,
@@ -961,13 +1047,7 @@
     for i in range(1, chunks):
         piece_map = state_product(chunk_maps[i], piece_map)
         piece_offset = state_product(chunk_maps[i], piece_offset) + chunk_offsets[i]
-    last_step = lax.axis_size("ctx") - 1
-    start_state = jnp.zeros_like(piece_offset)
-    for step in range(last_step):
-        moved = piece_offset
-        if step > 0:
-            moved = moved + state_product(piece_map, start_state)
-        start_state = passed_along(moved.astype(jnp.bfloat16), "ctx", 1).astype(jnp.float32)
+    start_state = chain(piece_map, piece_offset, True)
     starts = [start_state]
     for i in range(1, chunks):
         starts.append(state_product(chunk_maps[i - 1], starts[-1]) + chunk_offsets[i - 1])
@@ -1019,12 +1099,7 @@
     piece_reach = chunk_reach[chunks - 1]
     for i in range(chunks - 2, -1, -1):
         piece_reach = chunk_reach[i] + state_pull(chunk_maps[i], piece_reach)
-    last_grad = jnp.zeros_like(piece_reach)
-    for step in range(last_step):
-        moved = piece_reach
-        if step > 0:
-            moved = moved + state_pull(piece_map, last_grad)
-        last_grad = passed_along(moved.astype(jnp.bfloat16), "ctx", -1).astype(jnp.float32)
+    last_grad = chain(piece_map, piece_reach, False)
     lasts = [last_grad]
     for i in range(chunks - 1, 0, -1):
         lasts.insert(0, chunk_reach[i] + state_pull(chunk_maps[i], lasts[0]))

time: 430 us -> 410 us (0.953)
  Pallas kernels: 229 us -> 263 us
  waiting for transfers between devices: 70.1 us -> 38.3 us
  starting transfers between devices: 25.3 us -> 8.76 us
  matrix products: 32.8 us -> 28.4 us
    pallas_call x0 -> x2, Pallas kernels: none -> 43 us  [chain(): pl.pallas_call(functools.partial(chain_kernel, n, forward), in_specs=[vme...]
    ppermute x8 -> x2, waiting for transfers between devices: 41.5 us -> 2.44 us  [passed_along(): return lax.ppermute(block, axis, route)]
    ppermute x8 -> x2, starting transfers between devices: 19.2 us -> 2.57 us  [passed_along(): return lax.ppermute(block, axis, route)]
    pallas_call x1, Pallas kernels: 91.3 us -> 81.9 us  [scatter_sum(): pl.pallas_call(functools.partial(scatter_kernel, n, steps, widths), in_sp...]
    ppermute x2, waiting for transfers between devices: 0.23 us -> 5.44 us  [own_rows_sum(): total = total + lax.ppermute(sent, 'head', route).astype(jnp.float32)]
    dot_general x4 -> x0, matrix products: 4.65 us -> none  [the longest x2 2.8 us: state_pull(): jnp.einsum('hji,hjv->hiv', state_map, held, precision=highest_precision)]
    unnamed x89 -> x113, local copies, waits for them, and re-layouts: 9.96 us -> 9.34 us
  transfers between devices with their start and end apart: 16 -> 10, of which waited for: 12 -> 6; matrix products, arithmetic and copies ran while one was open for 14% -> 13% of each run, Pallas kernels for 51% -> 62%
where the time goes in v2:
time: 410 us; the launch traced here: 408 us
  Pallas kernels  263 us (64%)
  waiting for transfers between devices  38.3 us (9%)
  matrix products  28.4 us (7%)
  local copies, waits for them, and re-layouts  27.4 us (7%)
  other arithmetic  27.1 us (7%)
  between operations  15.1 us (4%)
  starting transfers between devices  8.76 us (2%)
    pallas_call x1, Pallas kernels, scatter_sum(): pl.pallas_call(functools.partial(scatter_kernel, n, steps, widths), in_sp...  81.9 us
    pallas_call x1, Pallas kernels, gather_all(): pl.pallas_call(functools.partial(gather_kernel, n), in_specs=[vmem] * 3,...  74.8 us
    pallas_call x4, Pallas kernels, per_head(): pl.pallas_call(kernel, grid=grid, in_specs=ins, out_specs=[spec for spec,...  48.8 us
    pallas_call x2, Pallas kernels, chain(): pl.pallas_call(functools.partial(chain_kernel, n, forward), in_specs=[vme...  43 us
    ppermute x3, waiting for transfers between devices, other_parts(): lax.ppermute(block, 'head', [(i, (i + shift) % parts) for i in range(part...  24.1 us
    dot_general x4, matrix products, mat_nn(): return jnp.dot(first_mat, second_mat, preferred_element_type=jnp.float32)  15.6 us
    pallas_call x2, Pallas kernels, outer_products(): pl.pallas_call(outer_kernel, grid=(features // block,), in_specs=specs, o...  14.7 us
    dot_general x4, matrix products, mat_nt(): lax.dot_general(first_mat, second_mat, (((1,), (1,)), ((), ())), preferre...  12.8 us
  transfers between devices with their start and end apart: 10, of which 6 were waited for; matrix products, arithmetic and copies ran while one was open for 13% of the time, Pallas kernels for 62%

profile of v2, /device:TPU:0, one launch (start us, length us, event | category | flops | bytes accessed | tf_op | source)
XLA Modules:
  0.0 408.2 jit_solution(9959108706119657372)
XLA Ops:
  11.5 3.1 collective-permute-start
  16.1 6.3 %collective-permute-done = bf16[32,5248]{1,0:T(8,128)(2,1)S(1)} collective-permute-done((bf16[32,5248]{1,0:T(8,128)(2,1)S(1)}, bf16[32,5248]{1,0:T(8,128)(2,1)S(1)}, u32[]{:S(2)}, u32[]{:S(2)}) %collective-permute-start) | collective-permute-done | bytes 335904 | tf_op jit(solution)/shard_map/ppermute | solution.py:331
  24.2 74.8 %shard_map.330 = (bf16[2,4,2,2,32,3082]{5,4,3,2,1,0:T(8,128)(2,1)}, bf16[2,128,1024]{2,1,0:T(8,128)(2,1)}, bf16[2,128,1024]{2,1,0:T(8,128)(2,1)}) custom-call(bf16[2,32,3082]{2,1,0:T(8,128)(2,1)} %pad_maximum_fusion.2.slab_ref, bf16[128,1024]{1,0:T(8,128)(2,1)} %bitcast.112, bf16[128,1024]{1,0:T(8,128)(2,1)} %bitcast.123), custom_call_target="tpu_custom_call" | custom-call | bytes 25247744 | tf_op jit(solution)/shard_map/pallas_call | solution.py:810
  102.9 5.0 %fusion.4.gate_ref = bf16[256,3080]{1,0:T(8,128)(2,1)S(1)} fusion(bf16[256,1024]{1,0:T(8,128)(2,1)S(1)} %fusion.35.refs_0_, bf16[1024,3082]{1,0:T(8,128)(2,1)} %bitcast.155), kind=kOutput, calls=%fused_computation.4 | convolution fusion | flops 1615595520 | bytes 8413184 | tf_op jit(solution)/shard_map/dot_general | solution.py:277
  112.2 2.3 multiply_add_fusion.q_ref.k_ref.v_ref
  114.5 23.2 %shard_map.331 = (f32[4,1,256,256]{3,2,1,0:T(8,128)}, f32[256,1024]{1,0:T(8,128)}, f32[256,512]{1,0:T(8,128)}, f32[4,1,128,128]{3,2,1,0:T(8,128)}, f32[4,1,128,256]{3,2,1,0:T(8,128)}) custom-call(f32[256,2048]{1,0:T(8,128)} %multiply_add_fusion.q_ref.k_ref.v_ref, f32[256,2048]{1,0:T(8,128)} %multiply_add_fusion.q_ref.k_ref.v_ref, ...), custom_call_target="tpu_custom_call" | custom-call | flops 6710886400 | bytes 6299648 | tf_op jit(solution)/shard_map/pallas_call | solution.py:232
  137.7 9.0 %shard_map.332 = f32[4,128,256]{2,1,0:T(8,128)} custom-call(f32[4,128,128]{2,1,0:T(8,128)} %bitcast.115, f32[4,128,256]{2,1,0:T(8,128)} %bitcast.121), custom_call_target="tpu_custom_call" | custom-call | bytes 4194304 | tf_op jit(solution)/shard_map/pallas_call | solution.py:924
  146.7 4.3 %shard_map.333.refs_1_ = bf16[256,1024]{1,0:T(8,128)(2,1)} custom-call(f32[256,1024]{1,0:T(8,128)} %get-tuple-element.47.o_ref, f32[256,512]{1,0:T(8,128)} %get-tuple-element.48.e_ref, f32[4,1,128,256]{3,2,1,0:T(8,128)} %bitcast.109, bf16[256,3080]{1,0:T(8,128)(2,1)} %copy-done.5, f32[1,1024]{1,0:T(1,128)} %bitcast.147), custom_call_target="tpu_custom_call" | custom-call | flops 402653184 | bytes 3678208 | tf_op jit(solution)/shard_map/pallas_call | solution.py:232
  151.0 2.5 fusion.23
  153.6 12.9 %collective-permute-done.2 = bf16[256,1024]{1,0:T(8,128)(2,1)S(1)} collective-permute-done((bf16[256,1024]{1,0:T(8,128)(2,1)S(1)}, bf16[256,1024]{1,0:T(8,128)(2,1)S(1)}, u32[]{:S(2)}, u32[]{:S(2)}) %collective-permute-start.2) | collective-permute-done | bytes 524320 | tf_op jit(solution)/shard_map/ppermute | solution.py:345
  167.0 4.6 %fusion.9 = f32[256,2816]{1,0:T(8,128)S(1)} fusion(bf16[256,1024]{1,0:T(8,128)(2,1)S(1)} %multiply_convert_fusion.2.refs_2_, bf16[1024,5248]{1,0:T(8,128)(2,1)} %bitcast.160), kind=kOutput, calls=%fused_computation.7 | convolution fusion | flops 1476395008 | bytes 9175040 | tf_op jit(solution)/shard_map/dot_general | solution.py:277
  172.8 2.4 fusion.21
  175.2 1.7 fusion.29
  178.5 10.5 %collective-permute-done.4 = bf16[256,1024]{1,0:T(8,128)(2,1)S(1)} collective-permute-done((bf16[256,1024]{1,0:T(8,128)(2,1)S(1)}, bf16[256,1024]{1,0:T(8,128)(2,1)S(1)}, u32[]{:S(2)}, u32[]{:S(2)}) %collective-permute-start.4) | collective-permute-done | bytes 524320 | tf_op jit(solution)/shard_map/ppermute | solution.py:345
  190.0 1.6 fusion.64
  191.6 8.4 %shard_map.339 = bf16[1024,5248]{1,0:T(8,128)(2,1)} custom-call(bf16[256,1024]{1,0:T(8,128)(2,1)} %get-tuple-element.155.refs_0_, bf16[256,1024]{1,0:T(8,128)(2,1)} %shard_map.333.refs_1_, bf16[256,1024]{1,0:T(8,128)(2,1)} %copy-done.12, bf16[256,2816]{1,0:T(8,128)(2,1)} %pad_maximum_fusion.1.refs_3_, bf16[256,1024]{1,0:T(8,128)(2,1)} %bitcast.113, ...), custom_call_target="tpu_custom_call" | custom-call | flops 2751463424 | bytes 10747904 | tf_op jit(solution)/shard_map/pallas_call | solution.py:854
  200.0 3.1 fusion.13
  206.1 5.4 %collective-permute-done.3 = bf16[128,1024]{1,0:T(8,128)(2,1)} collective-permute-done((bf16[128,1024]{1,0:T(8,128)(2,1)}, bf16[128,1024]{1,0:T(8,128)(2,1)}, u32[]{:S(2)}, u32[]{:S(2)}) %collective-permute-start.3) | collective-permute-done | bytes 262176 | tf_op jit(solution)/shard_map/ppermute | solution.py:367
  211.6 2.0 fusion.47
  213.5 3.7 fusion.26.grad_ref
  217.2 5.7 %shard_map.334 = (f32[256,1024]{1,0:T(8,128)}, bf16[256,1024]{1,0:T(8,128)(2,1)}, f32[1,1,1024]{2,1,0:T(1,128)}, f32[4,1,128,256]{3,2,1,0:T(8,128)}) custom-call(f32[256,1024]{1,0:T(8,128)} %get-tuple-element.47.o_ref, f32[256,512]{1,0:T(8,128)} %get-tuple-element.48.e_ref, f32[4,1,128,256]{3,2,1,0:T(8,128)} %bitcast.110, bf16[256,3080]{1,0:T(8,128)(2,1)} %copy-done.5, ...), custom_call_target="tpu_custom_call" | custom-call | flops 805306368 | bytes 4202496 | tf_op jit(solution)/shard_map/pallas_call | solution.py:232
  222.9 34.0 %shard_map.335 = f32[4,128,256]{2,1,0:T(8,128)} custom-call(f32[4,128,128]{2,1,0:T(8,128)} %bitcast.116, f32[4,128,256]{2,1,0:T(8,128)} %bitcast.120), custom_call_target="tpu_custom_call" | custom-call | bytes 4194304 | tf_op jit(solution)/shard_map/pallas_call | solution.py:924
  256.9 15.6 %shard_map.336 = (f32[256,512]{1,0:T(8,128)}, f32[256,512]{1,0:T(8,128)}, f32[256,1024]{1,0:T(8,128)}, f32[4,1,256,1]{3,2,1,0:T(8,128)}, f32[4,1,256,1]{3,2,1,0:T(8,128)}) custom-call(f32[256,2048]{1,0:T(8,128)} %multiply_add_fusion.q_ref.k_ref.v_ref, f32[256,2048]{1,0:T(8,128)} %multiply_add_fusion.q_ref.k_ref.v_ref, ...), custom_call_target="tpu_custom_call" | custom-call | flops 6710886400 | bytes 9445376 | tf_op jit(solution)/shard_map/pallas_call | solution.py:232
  272.5 1.9 reduce.1
  278.0 2.2 multiply_reduce_fusion.3
  285.5 2.4 collective-permute-done.5
  289.0 5.5 %fusion = f32[256,1024]{1,0:T(8,128)S(1)} fusion(bf16[256,3080]{1,0:T(8,128)(2,1)S(1)} %pad_maximum_fusion.refs_1_, bf16[1024,3082]{1,0:T(8,128)(2,1)} %bitcast.156), kind=kOutput, calls=%fused_computation | convolution fusion | flops 1614807040 | bytes 8937472 | tf_op jit(solution)/shard_map/dot_general | solution.py:265
  294.8 6.3 %shard_map.337 = bf16[1024,3080]{1,0:T(8,128)(2,1)} custom-call(bf16[256,1024]{1,0:T(8,128)(2,1)} %copy-done.10, bf16[256,3080]{1,0:T(8,128)(2,1)} %copy-done.6), custom_call_target="tpu_custom_call" | custom-call | flops 1614807040 | bytes 6307840 | tf_op jit(solution)/shard_map/pallas_call | solution.py:854
  301.3 2.0 collective-permute-start.7
  305.7 81.9 %shard_map.338 = (f32[4,16,512]{2,1,0:T(8,128)}, f32[4,16,512]{2,1,0:T(8,128)}, f32[4,16,1024]{2,1,0:T(8,128)}, f32[4,16,1024]{2,1,0:T(8,128)}, f32[4,16,8]{2,1,0:T(8,128)}, /*index=5*/f32[96,128]{1,0:T(8,128)}) custom-call(bf16[4,2,2,4,16,3080]{5,4,3,2,1,0:T(8,128)(2,1)} %bitcast.108, f32[96,128]{1,0:T(8,128)} %pad_bitcast_fusion.sm_ref), custom_call_target="tpu_custom_call" | custom-call | bytes 25231360 | tf_op jit(solution)/shard_map/pallas_call | solution.py:615
  394.9 1.6 slice.290
  396.6 2.1 fusion.66
  (203 shorter events, 45.3 us)
Async XLA Ops:
  7.2 7.4 %copy-start.38 = (bf16[32,16]{0,1:T(8,128)(2,1)S(1)}, bf16[32,16]{0,1:T(8,128)(2,1)}, u32[]{:S(2)}) copy-start(bf16[32,16]{0,1:T(8,128)(2,1)} %param.26) | copy-start | bytes 3076
  7.2 7.5 %copy-start.46 = (bf16[32]{0:T(256)(128)(2,1)S(1)}, bf16[32]{0:T(256)(128)(2,1)}, u32[]{:S(2)}) copy-start(bf16[32]{0:T(256)(128)(2,1)} %param.34) | copy-start | bytes 196
  7.2 7.5 %copy-start.47 = (bf16[32]{0:T(256)(128)(2,1)S(1)}, bf16[32]{0:T(256)(128)(2,1)}, u32[]{:S(2)}) copy-start(bf16[32]{0:T(256)(128)(2,1)} %param.21) | copy-start | bytes 196
  7.2 7.8 %copy-start.22 = (bf16[32,1024]{1,0:T(8,128)(2,1)S(1)}, bf16[32,1024]{1,0:T(8,128)(2,1)}, u32[]{:S(2)}) copy-start(bf16[32,1024]{1,0:T(8,128)(2,1)} %param.23) | copy-start | bytes 196612
  7.2 7.8 %copy-start.23 = (bf16[32,1024]{1,0:T(8,128)(2,1)S(1)}, bf16[32,1024]{1,0:T(8,128)(2,1)}, u32[]{:S(2)}) copy-start(bf16[32,1024]{1,0:T(8,128)(2,1)} %param.22) | copy-start | bytes 196612
  7.2 143.7 %all-gather.2.cloned.1.call-start = ((), (), s32[]{:S(2)}) async-start(), calls=%async_computation.1 | async-start | bytes 11419648 | tf_op jit(solution)/shard_map/all_gather | solution.py:337
  8.3 6.8 %copy-start.20 = (bf16[32,2048]{1,0:T(8,128)(2,1)S(1)}, bf16[32,2048]{1,0:T(8,128)(2,1)}, u32[]{:S(2)}) copy-start(bf16[32,2048]{1,0:T(8,128)(2,1)} %param.25) | copy-start | bytes 393220
  8.3 6.7 %copy-start.21 = (bf16[32,2048]{1,0:T(8,128)(2,1)S(1)}, bf16[32,2048]{1,0:T(8,128)(2,1)}, u32[]{:S(2)}) copy-start(bf16[32,2048]{1,0:T(8,128)(2,1)} %param.24) | copy-start | bytes 393220
  11.5 10.9 %collective-permute-start = (bf16[32,5248]{1,0:T(8,128)(2,1)S(1)}, bf16[32,5248]{1,0:T(8,128)(2,1)S(1)}, u32[]{:S(2)}, u32[]{:S(2)}) collective-permute-start(bf16[32,5248]{1,0:T(8,128)(2,1)S(1)} %get-tuple-element.170), channel_id=1, source_target_pairs={{0,16},{16,0},{1,17},{17,1},{2,18},{18,2},{3,19},{19,3},{4,20},{20... | collective-permute-start | bytes 1007624 | tf_op jit(solution)/shard_map/ppermute | solution.py:331
  15.0 8.5 %copy-start.41 = (bf16[1024]{0:T(1024)(128)(2,1)S(1)}, bf16[1024]{0:T(1024)(128)(2,1)}, u32[]{:S(2)}) copy-start(bf16[1024]{0:T(1024)(128)(2,1)} %param.32) | copy-start | bytes 6148
  15.1 9.1 %copy-start.48 = (f32[4]{0:T(128)S(1)}, f32[4]{0:T(128)}, u32[]{:S(2)}) copy-start(f32[4]{0:T(128)} %param.30) | copy-start | bytes 52
  15.1 9.1 %copy-start.30 = (bf16[4,1024]{1,0:T(4,128)(2,1)S(1)}, bf16[4,1024]{1,0:T(4,128)(2,1)}, u32[]{:S(2)}) copy-start(bf16[4,1024]{1,0:T(4,128)(2,1)} %param.29) | copy-start | bytes 24580
  15.1 9.1 %copy-start.35 = (bf16[4,512]{1,0:T(4,128)(2,1)S(1)}, bf16[4,512]{1,0:T(4,128)(2,1)}, u32[]{:S(2)}) copy-start(bf16[4,512]{1,0:T(4,128)(2,1)} %param.28) | copy-start | bytes 12292
  15.1 9.1 %copy-start.36 = (bf16[4,512]{1,0:T(4,128)(2,1)S(1)}, bf16[4,512]{1,0:T(4,128)(2,1)}, u32[]{:S(2)}) copy-start(bf16[4,512]{1,0:T(4,128)(2,1)} %param.27) | copy-start | bytes 12292
  23.5 371.5 %reduce-scatter.2.cloned.1.call-start = ((), (), s32[]{:S(2)}) async-start(), calls=%async_computation.2 | async-start | bytes 11419648 | tf_op jit(solution)/shard_map/reduce_scatter | solution.py:1111
  24.2 85.4 %copy-start.33 = (f32[4]{0:T(128)}, f32[4]{0:T(128)S(1)}, u32[]{:S(2)}) copy-start(f32[4]{0:T(128)S(1)} %exponential_negate_fusion) | copy-start | bytes 52
  102.8 6.7 %copy-start.31 = (f32[4]{0:T(128)S(1)}, f32[4]{0:T(128)}, u32[]{:S(2)}) copy-start(f32[4]{0:T(128)} %param.31) | copy-start | bytes 52
  107.9 4.0 collective-permute-start.1
  151.0 15.5 %copy-start.7 = (bf16[2,128,1024]{2,1,0:T(8,128)(2,1)S(1)}, bf16[2,128,1024]{2,1,0:T(8,128)(2,1)}, u32[]{:S(2)}) copy-start(bf16[2,128,1024]{2,1,0:T(8,128)(2,1)} %get-tuple-element.45) | copy-start | bytes 1572868
  153.5 13.0 %collective-permute-start.2 = (bf16[256,1024]{1,0:T(8,128)(2,1)S(1)}, bf16[256,1024]{1,0:T(8,128)(2,1)S(1)}, u32[]{:S(2)}, u32[]{:S(2)}) collective-permute-start(bf16[256,1024]{1,0:T(8,128)(2,1)S(1)} %fusion.23), channel_id=1, source_target_pairs={{0,16},{16,0},{1,17},{17,1},{2,18},{18,2},{3,19},{19,3},{4,20},{20... | collective-permute-start | bytes 1572872 | tf_op jit(solution)/shard_map/ppermute | solution.py:345
  176.9 12.1 %collective-permute-start.4 = (bf16[256,1024]{1,0:T(8,128)(2,1)S(1)}, bf16[256,1024]{1,0:T(8,128)(2,1)S(1)}, u32[]{:S(2)}, u32[]{:S(2)}) collective-permute-start(bf16[256,1024]{1,0:T(8,128)(2,1)S(1)} %fusion.29), channel_id=1, source_target_pairs={{0,16},{16,0},{1,17},{17,1},{2,18},{18,2},{3,19},{19,3},{4,20},{20... | collective-permute-start | bytes 1572872 | tf_op jit(solution)/shard_map/ppermute | solution.py:345
  204.9 6.7 %collective-permute-start.3 = (bf16[128,1024]{1,0:T(8,128)(2,1)}, bf16[128,1024]{1,0:T(8,128)(2,1)}, u32[]{:S(2)}, u32[]{:S(2)}) collective-permute-start(bf16[128,1024]{1,0:T(8,128)(2,1)} %dynamic-slice_convert_fusion.1), channel_id=1, source_target_pairs={{0,16},{16,0},{1,17},{17,1},{2,18},{18,2},{3,19},{19,3},{4,20},{20... | collective-permute-start | bytes 786440 | tf_op jit(solution)/shard_map/ppermute | solution.py:367
  205.6 11.7 %copy-start.42 = (f32[128]{0:T(128)}, f32[128]{0:T(128)S(1)}, u32[]{:S(2)}) copy-start(f32[128]{0:T(128)S(1)} %fusion.39) | copy-start | bytes 1540
  280.9 7.0 %collective-permute-start.5 = (f32[3,2048]{1,0:T(4,128)}, f32[3,2048]{1,0:T(4,128)S(1)}, u32[]{:S(2)}, u32[]{:S(2)}) collective-permute-start(f32[3,2048]{1,0:T(4,128)} %pad_add_fusion.1), channel_id=1, source_target_pairs={{4,0},{8,4},{12,8},{5,1},{9,5},{13,9},{6,2},{10,6},{14,10},{7,3},{... | collective-permute-start | bytes 73736 | tf_op jit(solution)/shard_map/ppermute | solution.py:20
  294.6 6.5 %collective-permute-start.6 = (bf16[128,1024]{1,0:T(8,128)(2,1)S(1)}, bf16[128,1024]{1,0:T(8,128)(2,1)S(1)}, u32[]{:S(2)}, u32[]{:S(2)}) collective-permute-start(bf16[128,1024]{1,0:T(8,128)(2,1)S(1)} %dynamic-slice_convert_fusion), channel_id=1, source_target_pairs={{0,16},{16,0},{1,17},{17,1},{2,18},{18,2},{3,19},{19,3},{4,20},{20... | collective-permute-start | bytes 786440 | tf_op jit(solution)/shard_map/ppermute | solution.py:367
  294.8 8.5 %copy-start.43 = (f32[128]{0:T(128)S(1)}, f32[128]{0:T(128)}, u32[]{:S(2)}) copy-start(f32[128]{0:T(128)} %copy-done.42) | copy-start | bytes 1540
  294.8 8.5 %copy-start.9 = (f32[256,1024]{1,0:T(8,128)S(1)}, f32[256,1024]{1,0:T(8,128)}, u32[]{:S(2)}) copy-start(f32[256,1024]{1,0:T(8,128)} %get-tuple-element.156) | copy-start | bytes 3145732
  301.3 3.7 collective-permute-start.7
  387.6 11.0 %copy-start.19 = (f32[4,16,512]{2,1,0:T(8,128)S(1)}, f32[4,16,512]{2,1,0:T(8,128)}, u32[]{:S(2)}) copy-start(f32[4,16,512]{2,1,0:T(8,128)} %get-tuple-element.64) | copy-start | bytes 393220
  387.6 11.7 %copy-start.18 = (f32[4,16,512]{2,1,0:T(8,128)S(1)}, f32[4,16,512]{2,1,0:T(8,128)}, u32[]{:S(2)}) copy-start(f32[4,16,512]{2,1,0:T(8,128)} %get-tuple-element.65) | copy-start | bytes 393220
  387.7 12.3 %copy-start.17 = (f32[4,16,1024]{2,1,0:T(8,128)S(1)}, f32[4,16,1024]{2,1,0:T(8,128)}, u32[]{:S(2)}) copy-start(f32[4,16,1024]{2,1,0:T(8,128)} %get-tuple-element.66) | copy-start | bytes 786436
  387.7 13.0 %copy-start.16 = (f32[4,16,1024]{2,1,0:T(8,128)S(1)}, f32[4,16,1024]{2,1,0:T(8,128)}, u32[]{:S(2)}) copy-start(f32[4,16,1024]{2,1,0:T(8,128)} %get-tuple-element.67) | copy-start | bytes 786436
  (28 other events, 119.8 us)
Sparse Core Ops, SparseCore 0:
  23.6 105.9 all-gather.1
  200.1 128.5 reduce-scatter.1
